TPU v7x, 32 devices: a whole 2x2x4 slice. The times are simulated.
32 devices in a mesh: sample: 4 (over z), row: 2 (over y), col: 4 (over x, core).
Axes of the slice: x: 2, y: 2, z: 4, core: 2. Of those that a mesh axis runs over, the one named last changes fastest.
Arguments:
- single: bfloat16 [2048, 384], P(('sample', 'row')), parts along dimension 0, may hold values from -16 to 16
- pair_bias: bfloat16 [64, 512, 512], P('sample', 'row', 'col'), parts along dimension 0, may hold values from -4 to 400
- token_mask: int32 [2048], P('sample'), parts along dimension 0, may hold values from 0 to 1, as said below
- norm_gain: float32 [384], replicated, may hold values from 0.25 to 1.75
- w_query: bfloat16 [384, 384], replicated, may hold values from -0.3125 to 0.3125
- query_bias: float32 [384], replicated, may hold values from -3 to 3
- w_key: bfloat16 [384, 384], replicated, may hold values from -0.3125 to 0.3125
- w_value: bfloat16 [384, 384], replicated, may hold values from -0.3125 to 0.3125
- w_gate: bfloat16 [384, 384], replicated, may hold values from -0.3125 to 0.3125
- w_out: bfloat16 [384, 384], P(None, 'col'), may hold values from -0.3125 to 0.3125
Outputs:
- updated: float32 [2048, 384], P(('sample', 'row'), 'col'), parts along dimension 0
There are 4 independent parts, one for each index of `sample`. A program takes and returns all parts, laid end to end along the dimension named above; an argument that names none is the same for every part. Nothing has to cross between parts.
Inputs may be any that keep to these rules, and one draw needn't show every extreme that they name: `token_mask`: 1 for a leading run of 64 or more tokens and 0 for every token after it.
All inputs are finite; a program needn't handle non-finite values.
Results may differ from a plain program's by a relative error of at most 0.0014.
Values may be sent and summed in bfloat16 or wider, within the bound.
No kernel may reach another device: no remote copies, remote signals or barrier semaphores. Data moves between devices by JAX's collectives and lax.ppermute only.
A program may use at most 128 MiB of HBM per device.

v0:
```python
import math

import jax
import jax.numpy as jnp
from jax import lax
from jax.sharding import PartitionSpec as P

D = 384
HEADS = 16


def layer_norm(single, norm_gain):
    values_f32 = single.astype(jnp.float32)
    row_mean = jnp.mean(values_f32, axis=1, keepdims=True)
    centered = values_f32 - row_mean
    row_var = jnp.mean(centered * centered, axis=1, keepdims=True)
    return (centered * lax.rsqrt(row_var + 1e-05) * norm_gain).astype(jnp.bfloat16)


def attend(query_rows, key_rows, value_rows, bias_block, mask_cols):
    row_count = query_rows.shape[0]
    col_count = key_rows.shape[0]
    query_heads = query_rows.reshape(row_count, HEADS, -1)
    key_heads = key_rows.reshape(col_count, HEADS, -1)
    value_heads = value_rows.reshape(col_count, HEADS, -1)
    logits = jnp.einsum("qhd,khd->hqk", query_heads, key_heads, preferred_element_type=jnp.float32)
    mask_term = (mask_cols.astype(jnp.float32) - 1.0) * 1000000.0
    logits = logits + bias_block.astype(jnp.float32) + mask_term[None, None, :]
    row_peak = jnp.max(logits, axis=2)
    exp_scores = jnp.exp(logits - row_peak[:, :, None])
    row_total = jnp.sum(exp_scores, axis=2)
    weighted = jnp.einsum(
        "hqk,khd->qhd",
        exp_scores.astype(jnp.bfloat16),
        value_heads,
        preferred_element_type=jnp.float32,
    )
    return (row_peak.T, row_total.T, weighted.reshape(row_count, -1))


def on_device(
    single, pair_bias, token_mask, norm_gain, w_query, query_bias, w_key, w_value, w_gate, w_out
):
    head_dim = D // HEADS
    inv_sqrt = 1.0 / math.sqrt(head_dim)
    tok_rows = single.shape[0]
    col_total = lax.axis_size("col")
    out_width = w_out.shape[1]
    col_pos = lax.axis_index("col")
    normed = layer_norm(single, norm_gain)
    query = (
        (jnp.dot(normed, w_query, preferred_element_type=jnp.float32) + query_bias) * inv_sqrt
    ).astype(jnp.bfloat16)
    gate_act = jax.nn.sigmoid(jnp.dot(normed, w_gate, preferred_element_type=jnp.float32))
    single_cols = lax.dynamic_slice_in_dim(single, col_pos * out_width, out_width, 1).astype(
        jnp.float32
    )
    key_local = jnp.dot(normed, w_key, preferred_element_type=jnp.float32).astype(jnp.bfloat16)
    value_local = jnp.dot(normed, w_value, preferred_element_type=jnp.float32).astype(jnp.bfloat16)
    key_all, value_all = (
        lax.all_gather(key_local, "row", axis=0, tiled=True),
        lax.all_gather(value_local, "row", axis=0, tiled=True),
    )
    sub_rows = tok_rows // col_total
    query_start = col_pos * sub_rows
    bias_panel = lax.all_to_all(pair_bias, "col", split_axis=1, concat_axis=2, tiled=True)
    key_rows, value_rows = (key_all, value_all)
    query_part = lax.dynamic_slice_in_dim(query, query_start, sub_rows, 0)
    gate_part = lax.dynamic_slice_in_dim(gate_act, query_start, sub_rows, 0)
    row_peak, row_total, weighted = attend(query_part, key_rows, value_rows, bias_panel, token_mask)
    attended = weighted / jnp.repeat(row_total, head_dim, axis=1)
    gated_part = (gate_part * attended).astype(jnp.bfloat16)
    gated_all = lax.all_gather(gated_part, "col", axis=0, tiled=True)
    result = single_cols + jnp.dot(gated_all, w_out, preferred_element_type=jnp.float32)
    return result


def solution(mesh):
    return jax.shard_map(
        on_device,
        mesh=mesh,
        in_specs=(
            P(("sample", "row"), None),
            P("sample", "row", "col"),
            P("sample"),
            P(),
            P(),
            P(),
            P(),
            P(),
            P(),
            P(None, "col"),
        ),
        out_specs=P(("sample", "row"), "col"),
        check_vma=False,
    )
```

profile of v0, /device:TPU:0, one launch (start us, length us, event | category | flops | bytes accessed | tf_op | source)
XLA Modules:
  0.0 40.1 jit_solution(15966717443112249602)
XLA Ops:
  0.0 2.9 %copy.31 = bf16[16,256,128]{2,0,1:T(8,128)(2,1)} copy(bf16[16,256,128]{2,1,0:T(8,128)(2,1)} %param.11) | data formatting | bytes 2097152 | tf_op args[1]
  3.0 4.4 %all-to-all-start = ((bf16[16,256,128]{2,0,1:T(8,128)(2,1)}), bf16[16,256,128]{2,0,1:T(8,128)(2,1)S(1)}, u32[]{:S(2)}, u32[]{:S(2)}) async-start(bf16[16,256,128]{2,0,1:T(8,128)(2,1)} %copy.31), calls=%async_computation | async-start | bytes 2097152 | tf_op jit(solution)/shard_map/all_to_all | solution.py:66
  7.3 0.1 convert_reduce_fusion
  7.5 0.2 fusion.7
  7.7 0.3 convolution_convert_fusion.1
  8.0 0.3 fusion.18
  8.4 0.3 convolution_convert_fusion
  8.8 8.5 %all_gather.9 = bf16[512,384]{1,0:T(8,128)(2,1)S(1)} all-gather(bf16[256,384]{1,0:T(8,128)(2,1)S(1)} %convolution_convert_fusion.1), channel_id=1, replica_groups=mesh['sample'=4,'row'=2,'col'=4] {'row'}, dimensions={0}, use_global_device_ids=true | all-gather | bytes 589824 | tf_op jit(solution)/shard_map/all_gather | solution.py:62
  17.3 0.2 copy.28
  17.5 0.1 copy.29
  17.6 7.3 %all_gather.10 = bf16[512,384]{1,0:T(8,128)(2,1)S(1)} all-gather(bf16[256,384]{1,0:T(8,128)(2,1)S(1)} %convolution_convert_fusion), channel_id=1, replica_groups=mesh['sample'=4,'row'=2,'col'=4] {'row'}, dimensions={0}, use_global_device_ids=true | all-gather | bytes 589824 | tf_op jit(solution)/shard_map/all_gather | solution.py:61
  24.9 0.2 copy.30
  25.1 0.1 constant_dynamic-slice_fusion
  25.3 0.1 copy.34
  25.4 1.1 %fusion.21 = f32[256,384]{1,0:T(8,128)} fusion(bf16[384,384]{1,0:T(8,128)(2,1)S(1)} %copy-done.3, bf16[256,384]{1,0:T(8,128)(2,1)S(1)} %copy-done.1, f32[384]{0:T(512)S(1)} %copy-done.5, f32[256]{0:T(256)S(1)} %add_rsqrt_fusion, f32[256]{0:T(256)S(1)} %broadcast_multiply_fusion), kind=kOutput, calls=%fused_computation.32 | convolution fusion | flops 75988992 | bytes 888320 | tf_op jit(solution)/shard_map/dot_general | solution.py:54
  26.5 2.2 %copy.36 = f32[16,4,64,128]{3,1,2,0:T(4,128)} copy(bf16[16,4,64,128]{3,0,2,1:T(8,128)(2,1)S(1)} %bitcast.24) | data formatting | bytes 3145728 | tf_op jit(solution)/shard_map/convert_element_type | solution.py:28
  28.6 2.1 %reshape.37 = f32[16,64,512]{2,1,0:T(8,128)S(1)} reshape(f32[16,64,4,128]{3,2,1,0:T(4,128)} %bitcast.23) | data formatting | bytes 4194304 | tf_op jit(solution)/shard_map/convert_element_type | solution.py:28
  30.7 0.6 %fusion.23 = (f32[16,64]{1,0:T(8,128)S(1)}, f32[16,64,512]{2,1,0:T(8,128)S(1)}) fusion(f32[512]{0:T(512)S(1)} %add_multiply_fusion, f32[16,64,512]{2,1,0:T(8,128)S(1)} %reshape.37, bf16[64,16,24]{0,2,1:T(8,128)(2,1)S(1)} %bitcast.28, bf16[512,16,24]{0,2,1:T(8,128)(2,1)S(1)} %bitcast.25), kind=kOutput, calls=%fused_computation.33 | convolution fusion | flops 26737664 | bytes 4642816 | tf_op jit(solution)/shard_map/qhd,khd->hqk/dot_general | solution.py:26
  31.3 0.8 %fusion = f32[16,64]{1,0:T(8,128)S(1)} fusion(f32[16,64,512]{2,1,0:T(8,128)S(1)} %get-tuple-element.6, f32[16,64]{1,0:T(8,128)S(1)} %get-tuple-element.5), kind=kLoop, calls=%fused_computation.3 | loop fusion | flops 1047552 | bytes 2105344 | tf_op jit(solution)/shard_map/reduce_sum | solution.py:31
  32.1 0.5 %fusion.2 = f32[64,16,24]{0,2,1:T(8,128)S(1)} fusion(bf16[512,16,24]{0,2,1:T(8,128)(2,1)S(1)} %bitcast.26, f32[16,64,512]{2,1,0:T(8,128)S(1)} %get-tuple-element.6, f32[16,64]{1,0:T(8,128)S(1)} %get-tuple-element.5, f32[64,16]{0,1:T(8,128)S(1)} %bitcast.29), kind=kOutput, calls=%fused_computation.8 | convolution fusion | flops 26238976 | bytes 2596864 | tf_op jit(solution)/shard_map/hqk,khd->qhd/dot_general | solution.py:32
  32.6 0.1 copy.33
  32.7 0.9 %fusion.16 = bf16[64,384]{1,0:T(8,128)(2,1)S(1)} fusion(f32[64,384]{1,0:T(8,128)S(1)} %copy.33, f32[256,384]{1,0:T(8,128)} %fusion.21, s32[]{:T(128)S(6)} %select_n.8), kind=kLoop, calls=%fused_computation.26 | loop fusion | flops 122880 | bytes 245764 | tf_op jit(solution)/shard_map/convert_element_type | solution.py:72
  33.7 5.6 %all_gather.11 = bf16[256,384]{1,0:T(8,128)(2,1)S(1)} all-gather(bf16[64,384]{1,0:T(8,128)(2,1)S(1)} %fusion.16), channel_id=1, replica_groups=mesh['sample'=4,'row'=2,'col'=4] {'col'}, dimensions={0}, use_global_device_ids=true | all-gather | bytes 245760 | tf_op jit(solution)/shard_map/all_gather | solution.py:73
  39.3 0.8 %convolution_add_fusion = f32[256,96]{0,1:T(8,128)} fusion(bf16[256,384]{1,0:T(8,128)(2,1)S(1)} %all_gather.11, bf16[384,96]{0,1:T(8,128)(2,1)S(1)} %copy-done.4, bf16[256,96]{0,1:T(8,128)(2,1)S(1)} %copy.34), kind=kOutput, calls=%fused_computation.9 | convolution fusion | flops 18923520 | bytes 417792 | tf_op jit(solution)/shard_map/dot_general | solution.py:74
  (23 shorter events, 0.1 us)
Async XLA Ops:
  0.0 7.7 %copy-start = (bf16[384,384]{1,0:T(8,128)(2,1)S(1)}, bf16[384,384]{1,0:T(8,128)(2,1)}, u32[]{:S(2)}) copy-start(bf16[384,384]{1,0:T(8,128)(2,1)} %param.17) | copy-start | bytes 884740
  0.0 7.3 %copy-start.1 = (bf16[256,384]{1,0:T(8,128)(2,1)S(1)}, bf16[256,384]{1,0:T(8,128)(2,1)}, u32[]{:S(2)}) copy-start(bf16[256,384]{1,0:T(8,128)(2,1)} %param.10) | copy-start | bytes 589828
  0.0 7.7 %copy-start.5 = (f32[384]{0:T(512)S(1)}, f32[384]{0:T(512)}, u32[]{:S(2)}) copy-start(f32[384]{0:T(512)} %param.13) | copy-start | bytes 4612
  3.0 5.1 %copy-start.2 = (bf16[384,384]{1,0:T(8,128)(2,1)S(1)}, bf16[384,384]{1,0:T(8,128)(2,1)}, u32[]{:S(2)}) copy-start(bf16[384,384]{1,0:T(8,128)(2,1)} %param.14) | copy-start | bytes 884740
  3.0 5.5 %copy-start.8 = (bf16[384,384]{1,0:T(8,128)(2,1)S(1)}, bf16[384,384]{1,0:T(8,128)(2,1)}, u32[]{:S(2)}) copy-start(bf16[384,384]{1,0:T(8,128)(2,1)} %param.16) | copy-start | bytes 884740
  3.0 5.8 %copy-start.6 = (f32[384]{0:T(512)S(1)}, f32[384]{0:T(512)}, u32[]{:S(2)}) copy-start(f32[384]{0:T(512)} %param.15) | copy-start | bytes 4612
  3.0 23.5 %all-to-all-start = ((bf16[16,256,128]{2,0,1:T(8,128)(2,1)}), bf16[16,256,128]{2,0,1:T(8,128)(2,1)S(1)}, u32[]{:S(2)}, u32[]{:S(2)}) async-start(bf16[16,256,128]{2,0,1:T(8,128)(2,1)} %copy.31), calls=%async_computation | async-start | bytes 2097152 | tf_op jit(solution)/shard_map/all_to_all | solution.py:66
  8.4 17.0 %copy-start.7 = (s32[512]{0:T(512)S(1)}, s32[512]{0:T(512)}, u32[]{:S(2)}) copy-start(s32[512]{0:T(512)} %param.12) | copy-start | bytes 6148
  8.4 17.0 %copy-start.3 = (bf16[384,384]{1,0:T(8,128)(2,1)S(1)}, bf16[384,384]{1,0:T(8,128)(2,1)}, u32[]{:S(2)}) copy-start(bf16[384,384]{1,0:T(8,128)(2,1)} %param.18) | copy-start | bytes 884740
  32.1 7.2 %copy-start.4 = (bf16[384,96]{0,1:T(8,128)(2,1)S(1)}, bf16[384,96]{0,1:T(8,128)(2,1)}, u32[]{:S(2)}) copy-start(bf16[384,96]{0,1:T(8,128)(2,1)} %param.19) | copy-start | bytes 221188
where the time goes:
time: 40.4 us; the launch traced here: 40.1 us
  blocking collectives  21.4 us (53%)
  local copies, waits for them, and re-layouts  8.06 us (20%)
  starting transfers between devices  4.38 us (11%)
  matrix products  4.02 us (10%)
  other arithmetic  2.06 us (5%)
    all_gather x1, blocking collectives, on_device(): lax.all_gather(value_local, 'row', axis=0, tiled=True)  8.47 us
    all_gather x1, blocking collectives, on_device(): lax.all_gather(key_local, 'row', axis=0, tiled=True)  7.34 us
    all_gather x1, blocking collectives, on_device(): gated_all = lax.all_gather(gated_part, 'col', axis=0, tiled=True)  5.6 us
    all_to_all x1, starting transfers between devices, on_device(): lax.all_to_all(pair_bias, 'col', split_axis=1, concat_axis=2, tiled=True)  4.38 us
    convert_element_type x2, local copies, waits for them, and re-layouts, attend(): logits = logits + bias_block.astype(jnp.float32) + mask_term[None, None, :]  4.25 us
    unnamed x20, local copies, waits for them, and re-layouts  3.08 us
    dot_general x1, matrix products, on_device(): jnp.dot(normed, w_gate, preferred_element_type=jnp.float32)  1.09 us
    convert_element_type x1, other arithmetic, on_device(): gated_part = (gate_part * attended).astype(jnp.bfloat16)  0.94 us
  transfers between devices with their start and end apart: 1, of which 0 were waited for; matrix products, arithmetic and copies ran while one was open for 8% of the time, Pallas kernels for 0%

commit v1 on v0

v1 whole, which is shorter than its diff:
```python
import functools
import math

import jax
import jax.numpy as jnp
from jax import lax
from jax.experimental import pallas as pl
from jax.experimental.pallas import tpu as pltpu
from jax.sharding import PartitionSpec as P

D = 384
HEADS = 16
EPS = 1e-05
HEAD_DIM = D // HEADS
SCALE = 1.0 / math.sqrt(HEAD_DIM)
NT = (((1,), (1,)), ((), ()))
F32 = jnp.float32
BF16 = jnp.bfloat16


def layer_norm(single, norm_gain):
    values_f32 = single.astype(jnp.float32)
    row_mean = jnp.mean(values_f32, axis=1, keepdims=True)
    centered = values_f32 - row_mean
    row_var = jnp.mean(centered * centered, axis=1, keepdims=True)
    return (centered * lax.rsqrt(row_var + EPS) * norm_gain).astype(jnp.bfloat16)


def attend(query_rows, key_rows, value_rows, bias_block, mask_cols):
    row_count = query_rows.shape[0]
    col_count = key_rows.shape[0]
    query_heads = query_rows.reshape(row_count, HEADS, -1)
    key_heads = key_rows.reshape(col_count, HEADS, -1)
    value_heads = value_rows.reshape(col_count, HEADS, -1)
    logits = jnp.einsum("qhd,khd->hqk", query_heads, key_heads, preferred_element_type=jnp.float32)
    mask_term = (mask_cols.astype(jnp.float32) - 1.0) * 1000000.0
    logits = logits + bias_block.astype(jnp.float32) + mask_term[None, None, :]
    row_peak = jnp.max(logits, axis=2)
    exp_scores = jnp.exp(logits - row_peak[:, :, None])
    row_total = jnp.sum(exp_scores, axis=2)
    weighted = jnp.einsum(
        "hqk,khd->qhd",
        exp_scores.astype(jnp.bfloat16),
        value_heads,
        preferred_element_type=jnp.float32,
    )
    return (row_total.T, weighted.reshape(row_count, -1))


def general_plan(
    single, pair_bias, token_mask, norm_gain, w_query, query_bias, w_key, w_value, w_gate, w_out
):
    tok_rows = single.shape[0]
    col_total = lax.axis_size("col")
    out_width = w_out.shape[1]
    col_pos = lax.axis_index("col")
    normed = layer_norm(single, norm_gain)
    query = (
        (jnp.dot(normed, w_query, preferred_element_type=jnp.float32) + query_bias) * SCALE
    ).astype(jnp.bfloat16)
    gate_act = jax.nn.sigmoid(jnp.dot(normed, w_gate, preferred_element_type=jnp.float32))
    single_cols = lax.dynamic_slice_in_dim(single, col_pos * out_width, out_width, 1).astype(
        jnp.float32
    )
    key_local = jnp.dot(normed, w_key, preferred_element_type=jnp.float32).astype(jnp.bfloat16)
    value_local = jnp.dot(normed, w_value, preferred_element_type=jnp.float32).astype(jnp.bfloat16)
    key_rows = lax.all_gather(key_local, "row", axis=0, tiled=True)
    value_rows = lax.all_gather(value_local, "row", axis=0, tiled=True)
    sub_rows = tok_rows // col_total
    query_start = col_pos * sub_rows
    bias_panel = lax.all_to_all(pair_bias, "col", split_axis=1, concat_axis=2, tiled=True)
    query_part = lax.dynamic_slice_in_dim(query, query_start, sub_rows, 0)
    gate_part = lax.dynamic_slice_in_dim(gate_act, query_start, sub_rows, 0)
    row_total, weighted = attend(query_part, key_rows, value_rows, bias_panel, token_mask)
    attended = weighted / jnp.repeat(row_total, HEAD_DIM, axis=1)
    gated_part = (gate_part * attended).astype(jnp.bfloat16)
    gated_all = lax.all_gather(gated_part, "col", axis=0, tiled=True)
    return single_cols + jnp.dot(gated_all, w_out, preferred_element_type=jnp.float32)


def place():
    col = lax.axis_index("col")
    row = lax.axis_index("row")
    chip = col // 2
    core = col % 2
    half = (chip + core) % 2
    return row, col, chip, core, half


def prepare_kernel(
    single_ref, gain_ref, wq_ref, bq_ref, wk_ref, wv_ref, wg_ref, wo_ref,
    q_ref, gate_ref, wkv_ref, wo_own_ref, wo_oth_ref, res_ref, tmp_ref,
):
    _, col, _, _, half = place()
    hd = D // 2
    width = wo_ref.shape[0]
    x = single_ref[...].astype(F32)
    normed = layer_norm(single_ref[...], gain_ref[...])
    query = (jnp.dot(normed, wq_ref[...], preferred_element_type=F32) + bq_ref[...]) * SCALE
    q_ref[...] = jnp.where(half == 0, query[:, :hd], query[:, hd:]).astype(BF16)
    n = x.shape[0]
    gate = jnp.dot(normed, wg_ref[...], preferred_element_type=F32)
    tmp_ref[:, :n] = gate.T
    gate_ref[...] = jax.nn.sigmoid(tmp_ref[pl.ds(pl.multiple_of(half * hd, 8), hd), :n])
    tmp_ref[:, :n] = x.T
    res_ref[...] = tmp_ref[pl.ds(pl.multiple_of(col * width, 8), width), :n]
    tmp_ref[...] = wk_ref[...].astype(F32).T
    wkv_ref[:hd, :] = tmp_ref[pl.ds(pl.multiple_of(half * hd, 8), hd), :].astype(BF16)
    tmp_ref[...] = wv_ref[...].astype(F32).T
    wkv_ref[hd:, :] = tmp_ref[pl.ds(pl.multiple_of(half * hd, 8), hd), :].astype(BF16)
    wo = wo_ref[...].astype(F32)
    wo_own_ref[...] = jnp.where(half == 0, wo[:, :hd], wo[:, hd:]).astype(BF16)
    wo_oth_ref[...] = jnp.where(half == 0, wo[:, hd:], wo[:, :hd]).astype(BF16)


def partial_kernel(
    recv_ref, own_ref, gain_ref, wkv_ref, q_ref, bias_ref, bias_in_ref, mask_ref,
    send_ref, att_ref, lse_ref, kv_ref,
):
    row, _, chip, core, half = place()
    hd = D // 2
    heads = HEADS // 2
    n_q = q_ref.shape[0]
    n_k = recv_ref.shape[0]
    blk = n_k // 2
    first = pl.multiple_of(core * blk, blk)
    second = pl.multiple_of((1 - core) * blk, blk)

    @pl.when(chip == row)
    def _():
        kv_ref[:blk, :] = own_ref[pl.ds(first, blk), :]
        kv_ref[blk:, :] = own_ref[pl.ds(second, blk), :]

    @pl.when(chip != row)
    def _():
        kv_ref[:blk, :] = recv_ref[pl.ds(first, blk), :]
        kv_ref[blk:, :] = recv_ref[pl.ds(second, blk), :]

    base = chip * n_k
    mask_a = mask_ref[:, pl.ds(pl.multiple_of(base + first, blk), blk)]
    mask_b = mask_ref[:, pl.ds(pl.multiple_of(base + second, blk), blk)]
    mask_a = (mask_a.astype(F32) - 1.0) * 1000000.0
    mask_b = (mask_b.astype(F32) - 1.0) * 1000000.0
    normed = layer_norm(kv_ref[...], gain_ref[...])
    kv_t = lax.dot_general(wkv_ref[...], normed, NT, preferred_element_type=F32)
    key_t = kv_t[:hd].astype(BF16)
    query = q_ref[...]
    feature = lax.broadcasted_iota(jnp.int32, (1, hd), 1)
    lane = lax.broadcasted_iota(jnp.int32, (n_q, 128), 1)
    peaks = jnp.zeros((n_q, 128), F32)
    ones = jnp.ones((8, n_k), F32)
    sums = []
    for h in range(heads):
        lo = h * HEAD_DIM
        own_feat = ((feature >= lo) & (feature < lo + HEAD_DIM)).astype(F32).astype(BF16)
        logits = jnp.dot(query * own_feat, key_t, preferred_element_type=F32)
        la = logits[:, :blk] + bias_ref[half * heads + h].astype(F32) + mask_a
        lb = logits[:, blk:] + bias_in_ref[h].astype(F32) + mask_b
        peak = jnp.max(jnp.maximum(la, lb), axis=1, keepdims=True)
        probs = jnp.concatenate([jnp.exp(la - peak), jnp.exp(lb - peak)], axis=1).astype(BF16)
        value = jnp.concatenate([kv_t[hd + lo : hd + lo + HEAD_DIM], ones], axis=0).astype(BF16)
        out = lax.dot_general(value, probs, NT, preferred_element_type=F32)
        total = out[HEAD_DIM : HEAD_DIM + 1]
        att = out[:HEAD_DIM] / total
        att_ref[lo : lo + HEAD_DIM, :] = att
        sums.append(total)
        peaks = jnp.where(lane == h, peak, peaks)
    lse = peaks.T[:heads] + jnp.log(jnp.concatenate(sums, axis=0))
    lse_ref[...] = lse
    hi = lse.astype(BF16)
    rest = lse - hi.astype(F32)
    mid = rest.astype(BF16)
    low = (rest - mid.astype(F32)).astype(BF16)
    send_ref[:hd, :] = att_ref[...].astype(BF16)
    send_ref[hd : hd + heads, :] = hi
    send_ref[hd + heads : hd + 2 * heads, :] = mid
    send_ref[hd + 2 * heads :, :] = low


def merge_kernel(recv_ref, att_ref, lse_ref, gate_ref, gated_ref):
    hd = D // 2
    heads = HEADS // 2
    parts = recv_ref[hd:, :].astype(F32)
    other = parts[:heads] + parts[heads : 2 * heads] + parts[2 * heads :]
    own = lse_ref[...]
    top = jnp.maximum(own, other)
    w_own = jnp.exp(own - top)
    w_oth = jnp.exp(other - top)
    inv = 1.0 / (w_own + w_oth)
    w_own = w_own * inv
    w_oth = w_oth * inv
    pieces = []
    for h in range(heads):
        rows = slice(h * HEAD_DIM, (h + 1) * HEAD_DIM)
        att = w_own[h : h + 1] * att_ref[rows, :] + w_oth[h : h + 1] * recv_ref[rows, :].astype(F32)
        pieces.append(gate_ref[rows, :] * att)
    gated_ref[...] = jnp.concatenate(pieces, axis=0).astype(BF16)


def project_kernel(own_ref, oth_ref, wo_own_ref, wo_oth_ref, res_ref, out_ref):
    out_ref[...] = (
        res_ref[...]
        + jnp.dot(wo_own_ref[...], own_ref[...], preferred_element_type=F32)
        + jnp.dot(wo_oth_ref[...], oth_ref[...], preferred_element_type=F32)
    )


def call(kernel, outs, args, scratch=(), flops=0, trans=0):
    vmem = pl.BlockSpec(memory_space=pltpu.VMEM)
    nbytes = sum(math.prod(a.shape) * a.dtype.itemsize for a in (*args, *outs))
    return pl.pallas_call(
        kernel,
        out_shape=tuple(outs),
        in_specs=[vmem] * len(args),
        out_specs=tuple([vmem] * len(outs)),
        scratch_shapes=list(scratch),
        cost_estimate=pl.CostEstimate(flops=flops, bytes_accessed=nbytes, transcendentals=trans),
    )(*args)


def paired_plan(
    single, pair_bias, token_mask, norm_gain, w_query, query_bias, w_key, w_value, w_gate, w_out
):
    n = single.shape[0]
    heads, rows, cols = pair_bias.shape
    width = w_out.shape[1]
    hd = D // 2
    half_heads = heads // 2
    _, _, _, _, half = place()
    shape = jax.ShapeDtypeStruct
    swap_row = [(r * 4 + c, (1 - r) * 4 + (c ^ 1)) for r in range(2) for c in range(4)]
    swap_core = [(c, c ^ 1) for c in range(4)]
    swap_chip = [(c, c ^ 3) for c in range(4)]

    gain = norm_gain.reshape(1, D)
    single_in = lax.ppermute(single, ("row", "col"), swap_row)
    bias_out = lax.dynamic_slice_in_dim(pair_bias, (1 - half) * half_heads, half_heads, 0)
    bias_in = lax.ppermute(bias_out, "col", swap_core)
    query, gate, wkv, wo_own, wo_oth, res = call(
        prepare_kernel,
        [
            shape((n, hd), BF16),
            shape((hd, n), F32),
            shape((D, D), BF16),
            shape((width, hd), BF16),
            shape((width, hd), BF16),
            shape((width, n), F32),
        ],
        (single, gain, w_query, query_bias.reshape(1, D), w_key, w_value, w_gate, w_out.T),
        [pltpu.VMEM((D, D), F32)],
        flops=4 * n * D * D,
    )
    send, att, lse = call(
        partial_kernel,
        [
            shape((hd + 3 * half_heads, n), BF16),
            shape((hd, n), F32),
            shape((half_heads, n), F32),
        ],
        (single_in, single, gain, wkv, query, pair_bias, bias_in, token_mask.reshape(1, -1)),
        [pltpu.VMEM((n, D), BF16)],
        flops=4 * n * D * D,
        trans=half_heads * n * n,
    )
    recv = lax.ppermute(send, "col", swap_chip)
    (gated_own,) = call(merge_kernel, [shape((hd, n), BF16)], (recv, att, lse, gate), flops=n * D)
    gated_oth = lax.ppermute(gated_own, "col", swap_core)
    (out,) = call(
        project_kernel,
        [shape((width, n), F32)],
        (gated_own, gated_oth, wo_own, wo_oth, res),
        flops=2 * n * D * width,
    )
    return out.T


def on_device(single, pair_bias, *rest):
    heads, rows, cols = pair_bias.shape
    paired = (
        lax.axis_size("row") == 2
        and lax.axis_size("col") == 4
        and heads == HEADS
        and rows == single.shape[0]
        and 2 * cols == rows
        and cols % 128 == 0
    )
    plan = paired_plan if paired else general_plan
    return plan(single, pair_bias, *rest)


def solution(mesh):
    return jax.shard_map(
        on_device,
        mesh=mesh,
        in_specs=(
            P(("sample", "row"), None),
            P("sample", "row", "col"),
            P("sample"),
            P(),
            P(),
            P(),
            P(),
            P(),
            P(),
            P(None, "col"),
        ),
        out_specs=P(("sample", "row"), "col"),
        check_vma=False,
    )
```

time: 40.4 us -> 26.6 us (0.66)
  blocking collectives: 21.4 us -> 0 us
  Pallas kernels: 0 us -> 11.1 us
  waiting for transfers between devices: 0.01 us -> 6.2 us
  matrix products: 4.02 us -> 0 us
  local copies, waits for them, and re-layouts: 8.06 us -> 4.4 us
  other arithmetic: 2.06 us -> 0 us
    all_gather x3 -> x0, blocking collectives: 21.4 us -> none  [the longest x1 8.47 us: on_device(): lax.all_gather(value_local, 'row', axis=0, tiled=True)]
    pallas_call x0 -> x4, Pallas kernels: none -> 11.1 us  [call(): pl.pallas_call(kernel, out_shape=tuple(outs), in_specs=[vmem] * len(args)...]
    ppermute x0 -> x4, waiting for transfers between devices: none -> 6.2 us  [the longest x1 3.89 us: paired_plan(): recv = lax.ppermute(send, 'col', swap_chip)]
    ppermute x0 -> x4, starting transfers between devices: none -> 4.67 us  [the longest x1 2.62 us: paired_plan(): single_in = lax.ppermute(single, ('row', 'col'), swap_row)]
    all_to_all x1 -> x0, starting transfers between devices: 4.38 us -> none  [on_device(): lax.all_to_all(pair_bias, 'col', split_axis=1, concat_axis=2, tiled=True)]
    convert_element_type x2 -> x0, local copies, waits for them, and re-layouts: 4.25 us -> none  [attend(): logits = logits + bias_block.astype(jnp.float32) + mask_term[None, None, :]]
    dot_general x7 -> x0, matrix products: 4.02 us -> none  [the longest x1 1.09 us: on_device(): jnp.dot(normed, w_gate, preferred_element_type=jnp.float32)]
    reshape x0 -> x2, local copies, waits for them, and re-layouts: none -> 1.15 us  [the longest x1 0.59 us: paired_plan(): gain = norm_gain.reshape(1, D)]
  transfers between devices with their start and end apart: 1 -> 4, of which waited for: 0 -> 3; matrix products, arithmetic and copies ran while one was open for 8% -> 4% of each run, Pallas kernels for 0% -> 12%
where the time goes in v1:
time: 26.6 us; the launch traced here: 26.4 us
  Pallas kernels  11.1 us (42%)
  waiting for transfers between devices  6.2 us (23%)
  starting transfers between devices  4.67 us (18%)
  local copies, waits for them, and re-layouts  4.4 us (17%)
    pallas_call x4, Pallas kernels, call(): pl.pallas_call(kernel, out_shape=tuple(outs), in_specs=[vmem] * len(args)...  11.1 us
    ppermute x1, waiting for transfers between devices, paired_plan(): recv = lax.ppermute(send, 'col', swap_chip)  3.89 us
    ppermute x1, starting transfers between devices, paired_plan(): single_in = lax.ppermute(single, ('row', 'col'), swap_row)  2.62 us
    unnamed x14, local copies, waits for them, and re-layouts  2.13 us
    ppermute x1, waiting for transfers between devices, paired_plan(): gated_oth = lax.ppermute(gated_own, 'col', swap_core)  1.4 us
    ppermute x1, starting transfers between devices, paired_plan(): recv = lax.ppermute(send, 'col', swap_chip)  1.38 us
    dynamic_slice x1, local copies, waits for them, and re-layouts, paired_plan(): lax.dynamic_slice_in_dim(pair_bias, (1 - half) * half_heads, half_heads, 0)  1.12 us
    ppermute x1, waiting for transfers between devices, paired_plan(): single_in = lax.ppermute(single, ('row', 'col'), swap_row)  0.91 us
  transfers between devices with their start and end apart: 4, of which 3 were waited for; matrix products, arithmetic and copies ran while one was open for 4% of the time, Pallas kernels for 12%

profile of v1, /device:TPU:0, one launch (start us, length us, event | category | flops | bytes accessed | tf_op | source)
XLA Modules:
  0.0 26.4 jit_solution(3024518642235525110)
XLA Ops:
  0.0 0.0 copy-start
  0.0 1.1 %constant_dynamic-slice_fusion = bf16[8,256,128]{2,1,0:T(8,128)(2,1)S(1)} fusion(bf16[16,256,128]{2,1,0:T(8,128)(2,1)} %bias_ref.1, s32[]{:T(128)S(6)} %select_n.21), kind=kLoop, calls=%fused_computation | loop fusion | bytes 1048580 | tf_op jit(solution)/shard_map/dynamic_slice | solution.py:237
  1.1 0.0 copy-start.6
  1.1 0.6 %collective-permute-start.1 = (bf16[8,256,128]{2,1,0:T(8,128)(2,1)S(1)}, bf16[8,256,128]{2,1,0:T(8,128)(2,1)S(1)}, u32[]{:S(2)}, u32[]{:S(2)}) collective-permute-start(bf16[8,256,128]{2,1,0:T(8,128)(2,1)S(1)} %constant_dynamic-slice_fusion), channel_id=1, source_target_pairs={{0,1},{1,0},{2,3},{3,2},{4,5},{5,4},{6,7},{7,6},{8,9},{9,8},{10,11... | collective-permute-start | bytes 1572872 | tf_op jit(solution)/shard_map/ppermute | solution.py:238
  1.7 0.0 copy-done
  1.7 2.6 %collective-permute-start = (bf16[256,384]{1,0:T(8,128)(2,1)S(1)}, bf16[256,384]{1,0:T(8,128)(2,1)S(1)}, u32[]{:S(2)}, u32[]{:S(2)}) collective-permute-start(bf16[256,384]{1,0:T(8,128)(2,1)S(1)} %copy-done), channel_id=1, source_target_pairs={{0,5},{1,4},{2,7},{3,6},{4,1},{5,0},{6,3},{7,2},{8,13},{9,12},{10,... | collective-permute-start | bytes 589832 | tf_op jit(solution)/shard_map/ppermute | solution.py:236
  4.3 0.0 copy-done.5
  4.3 0.6 %reshape.9.gain_ref = f32[1,384]{1,0:T(1,128)} reshape(f32[384]{0:T(512)S(1)} %copy-done.5) | data formatting | bytes 3072 | tf_op jit(solution)/shard_map/reshape | solution.py:235
  4.9 0.0 copy-done.6
  4.9 0.6 %reshape.10.bq_ref = f32[1,384]{1,0:T(1,128)} reshape(f32[384]{0:T(512)S(1)} %copy-done.6) | data formatting | bytes 3072 | tf_op jit(solution)/shard_map/reshape | solution.py:249
  5.5 3.1 %shard_map.100 = (bf16[256,192]{1,0:T(8,128)(2,1)}, f32[192,256]{1,0:T(8,128)}, bf16[384,384]{1,0:T(8,128)(2,1)}, bf16[96,192]{1,0:T(8,128)(2,1)}, bf16[96,192]{1,0:T(8,128)(2,1)}, /*index=5*/f32[96,256]{1,0:T(8,128)}) custom-call(bf16[256,384]{1,0:T(8,128)(2,1)} %own_ref.1, f32[1,384]{1,0:T(1,128)} %reshape.9.gain_ref, bf16[384,384]{1,0:T(8,128)(2,1)} %wq_ref.1, ...), custom_call_target="tpu_custom_call" | custom-call | flops 150994944 | bytes 2214912 | tf_op jit(solution)/shard_map/pallas_call | solution.py:211
  8.6 0.9 %collective-permute-done.recv_ref = bf16[256,384]{1,0:T(8,128)(2,1)S(1)} collective-permute-done((bf16[256,384]{1,0:T(8,128)(2,1)S(1)}, bf16[256,384]{1,0:T(8,128)(2,1)S(1)}, u32[]{:S(2)}, u32[]{:S(2)}) %collective-permute-start) | collective-permute-done | bytes 196640 | tf_op jit(solution)/shard_map/ppermute | solution.py:236
  9.5 0.0 collective-permute-done.1.bias_in_ref
  9.5 0.7 %copy-done.2 = bf16[256,384]{1,0:T(8,128)(2,1)} copy-done((bf16[256,384]{1,0:T(8,128)(2,1)}, bf16[256,384]{1,0:T(8,128)(2,1)S(1)}, u32[]{:S(2)}) %copy-start.2) | copy-done | bytes 196632
  10.2 0.2 copy-done.1
  10.4 4.3 %shard_map.101 = (bf16[216,256]{1,0:T(8,128)(2,1)}, f32[192,256]{1,0:T(8,128)}, f32[8,256]{1,0:T(8,128)}) custom-call(bf16[256,384]{1,0:T(8,128)(2,1)} %copy-done.2, bf16[256,384]{1,0:T(8,128)(2,1)} %own_ref.1, f32[1,384]{1,0:T(1,128)} %reshape.9.gain_ref, bf16[384,384]{1,0:T(8,128)(2,1)} %get-tuple-element.14.wkv_ref, ...), custom_call_target="tpu_custom_call" | custom-call | flops 150994944 | bytes 2678272 | tf_op jit(solution)/shard_map/pallas_call | solution.py:211
  14.7 1.4 %collective-permute-start.2 = (bf16[216,256]{1,0:T(8,128)(2,1)}, bf16[216,256]{1,0:T(8,128)(2,1)S(1)}, u32[]{:S(2)}, u32[]{:S(2)}) collective-permute-start(bf16[216,256]{1,0:T(8,128)(2,1)} %get-tuple-element.16), channel_id=1, source_target_pairs={{0,3},{1,2},{2,1},{3,0},{4,7},{5,6},{6,5},{7,4},{8,11},{9,10},{10,... | collective-permute-start | bytes 331784 | tf_op jit(solution)/shard_map/ppermute | solution.py:265
  16.1 3.9 %collective-permute-done.2.recv_ref = bf16[216,256]{1,0:T(8,128)(2,1)S(1)} collective-permute-done((bf16[216,256]{1,0:T(8,128)(2,1)}, bf16[216,256]{1,0:T(8,128)(2,1)S(1)}, u32[]{:S(2)}, u32[]{:S(2)}) %collective-permute-start.2) | collective-permute-done | bytes 110624 | tf_op jit(solution)/shard_map/ppermute | solution.py:265
  19.9 0.6 %copy-done.3 = bf16[216,256]{1,0:T(8,128)(2,1)} copy-done((bf16[216,256]{1,0:T(8,128)(2,1)}, bf16[216,256]{1,0:T(8,128)(2,1)S(1)}, u32[]{:S(2)}) %copy-start.3) | copy-done | bytes 110616
  20.6 1.8 %shard_map.102.own_ref = bf16[192,256]{1,0:T(8,128)(2,1)} custom-call(bf16[216,256]{1,0:T(8,128)(2,1)} %copy-done.3, f32[192,256]{1,0:T(8,128)} %get-tuple-element.17.att_ref, f32[8,256]{1,0:T(8,128)} %get-tuple-element.18.lse_ref, f32[192,256]{1,0:T(8,128)} %get-tuple-element.19.gate_ref), custom_call_target="tpu_custom_call" | custom-call | flops 98304 | bytes 610304 | tf_op jit(solution)/shard_map/pallas_call | solution.py:211
  22.4 0.1 collective-permute-start.3
  22.5 1.4 %collective-permute-done.3.oth_ref = bf16[192,256]{1,0:T(8,128)(2,1)S(1)} collective-permute-done((bf16[192,256]{1,0:T(8,128)(2,1)}, bf16[192,256]{1,0:T(8,128)(2,1)S(1)}, u32[]{:S(2)}, u32[]{:S(2)}) %collective-permute-start.3) | collective-permute-done | bytes 98336 | tf_op jit(solution)/shard_map/ppermute | solution.py:267
  23.9 0.6 %copy-done.4 = bf16[192,256]{1,0:T(8,128)(2,1)} copy-done((bf16[192,256]{1,0:T(8,128)(2,1)}, bf16[192,256]{1,0:T(8,128)(2,1)S(1)}, u32[]{:S(2)}) %copy-start.4) | copy-done | bytes 98328
  24.5 1.9 %shard_map.103 = f32[96,256]{1,0:T(8,128)} custom-call(bf16[192,256]{1,0:T(8,128)(2,1)} %shard_map.102.own_ref, bf16[192,256]{1,0:T(8,128)(2,1)} %copy-done.4, bf16[96,192]{1,0:T(8,128)(2,1)} %get-tuple-element.20.wo_own_ref, bf16[96,192]{1,0:T(8,128)(2,1)} %get-tuple-element.21.wo_oth_ref, f32[96,256]{1,0:T(8,128)} %get-tuple-element.22.res_ref), custom_call_target="tpu_custom_call" | custom-call | flops 18874368 | bytes 466944 | tf_op jit(solution)/shard_map/pallas_call | solution.py:211
  (5 shorter events, 0.0 us)
Async XLA Ops:
  0.0 1.7 %copy-start = (bf16[256,384]{1,0:T(8,128)(2,1)S(1)}, bf16[256,384]{1,0:T(8,128)(2,1)}, u32[]{:S(2)}) copy-start(bf16[256,384]{1,0:T(8,128)(2,1)} %own_ref.1) | copy-start | bytes 589828
  0.0 4.3 %copy-start.5 = (f32[384]{0:T(512)S(1)}, f32[384]{0:T(512)}, u32[]{:S(2)}) copy-start(f32[384]{0:T(512)} %param.13) | copy-start | bytes 4612
  1.1 3.8 %copy-start.6 = (f32[384]{0:T(512)S(1)}, f32[384]{0:T(512)}, u32[]{:S(2)}) copy-start(f32[384]{0:T(512)} %param.15) | copy-start | bytes 4612
  1.1 8.4 %collective-permute-start.1 = (bf16[8,256,128]{2,1,0:T(8,128)(2,1)S(1)}, bf16[8,256,128]{2,1,0:T(8,128)(2,1)S(1)}, u32[]{:S(2)}, u32[]{:S(2)}) collective-permute-start(bf16[8,256,128]{2,1,0:T(8,128)(2,1)S(1)} %constant_dynamic-slice_fusion), channel_id=1, source_target_pairs={{0,1},{1,0},{2,3},{3,2},{4,5},{5,4},{6,7},{7,6},{8,9},{9,8},{10,11... | collective-permute-start | bytes 1572872 | tf_op jit(solution)/shard_map/ppermute | solution.py:238
  1.7 7.8 %collective-permute-start = (bf16[256,384]{1,0:T(8,128)(2,1)S(1)}, bf16[256,384]{1,0:T(8,128)(2,1)S(1)}, u32[]{:S(2)}, u32[]{:S(2)}) collective-permute-start(bf16[256,384]{1,0:T(8,128)(2,1)S(1)} %copy-done), channel_id=1, source_target_pairs={{0,5},{1,4},{2,7},{3,6},{4,1},{5,0},{6,3},{7,2},{8,13},{9,12},{10,... | collective-permute-start | bytes 589832 | tf_op jit(solution)/shard_map/ppermute | solution.py:236
  9.5 0.7 %copy-start.2 = (bf16[256,384]{1,0:T(8,128)(2,1)}, bf16[256,384]{1,0:T(8,128)(2,1)S(1)}, u32[]{:S(2)}) copy-start(bf16[256,384]{1,0:T(8,128)(2,1)S(1)} %collective-permute-done.recv_ref) | copy-start | bytes 589828
  9.5 0.9 %copy-start.1 = (bf16[8,256,128]{2,1,0:T(8,128)(2,1)}, bf16[8,256,128]{2,1,0:T(8,128)(2,1)S(1)}, u32[]{:S(2)}) copy-start(bf16[8,256,128]{2,1,0:T(8,128)(2,1)S(1)} %collective-permute-done.1.bias_in_ref) | copy-start | bytes 1572868
  14.7 5.3 %collective-permute-start.2 = (bf16[216,256]{1,0:T(8,128)(2,1)}, bf16[216,256]{1,0:T(8,128)(2,1)S(1)}, u32[]{:S(2)}, u32[]{:S(2)}) collective-permute-start(bf16[216,256]{1,0:T(8,128)(2,1)} %get-tuple-element.16), channel_id=1, source_target_pairs={{0,3},{1,2},{2,1},{3,0},{4,7},{5,6},{6,5},{7,4},{8,11},{9,10},{10,... | collective-permute-start | bytes 331784 | tf_op jit(solution)/shard_map/ppermute | solution.py:265
  19.9 0.6 %copy-start.3 = (bf16[216,256]{1,0:T(8,128)(2,1)}, bf16[216,256]{1,0:T(8,128)(2,1)S(1)}, u32[]{:S(2)}) copy-start(bf16[216,256]{1,0:T(8,128)(2,1)S(1)} %collective-permute-done.2.recv_ref) | copy-start | bytes 331780
  22.4 1.5 %collective-permute-start.3 = (bf16[192,256]{1,0:T(8,128)(2,1)}, bf16[192,256]{1,0:T(8,128)(2,1)S(1)}, u32[]{:S(2)}, u32[]{:S(2)}) collective-permute-start(bf16[192,256]{1,0:T(8,128)(2,1)} %shard_map.102.own_ref), channel_id=1, source_target_pairs={{0,1},{1,0},{2,3},{3,2},{4,5},{5,4},{6,7},{7,6},{8,9},{9,8},{10,11... | collective-permute-start | bytes 294920 | tf_op jit(solution)/shard_map/ppermute | solution.py:267
  23.9 0.6 %copy-start.4 = (bf16[192,256]{1,0:T(8,128)(2,1)}, bf16[192,256]{1,0:T(8,128)(2,1)S(1)}, u32[]{:S(2)}) copy-start(bf16[192,256]{1,0:T(8,128)(2,1)S(1)} %collective-permute-done.3.oth_ref) | copy-start | bytes 294916

commit v2 on v1

--- a/solution.py
+++ b/solution.py
@@ -95,8 +95,8 @@
     hd = D // 2
     width = wo_ref.shape[0]
     x = single_ref[...].astype(F32)
-    normed = layer_norm(single_ref[...], gain_ref[...])
-    query = (jnp.dot(normed, wq_ref[...], preferred_element_type=F32) + bq_ref[...]) * SCALE
+    normed = layer_norm(single_ref[...], gain_ref[...][None, :])
+    query = (jnp.dot(normed, wq_ref[...], preferred_element_type=F32) + bq_ref[...][None, :]) * SCALE
     q_ref[...] = jnp.where(half == 0, query[:, :hd], query[:, hd:]).astype(BF16)
     n = x.shape[0]
     gate = jnp.dot(normed, wg_ref[...], preferred_element_type=F32)
@@ -141,7 +141,7 @@
     mask_b = mask_ref[:, pl.ds(pl.multiple_of(base + second, blk), blk)]
     mask_a = (mask_a.astype(F32) - 1.0) * 1000000.0
     mask_b = (mask_b.astype(F32) - 1.0) * 1000000.0
-    normed = layer_norm(kv_ref[...], gain_ref[...])
+    normed = layer_norm(kv_ref[...], gain_ref[...][None, :])
     kv_t = lax.dot_general(wkv_ref[...], normed, NT, preferred_element_type=F32)
     key_t = kv_t[:hd].astype(BF16)
     query = q_ref[...]
@@ -155,7 +155,7 @@
         own_feat = ((feature >= lo) & (feature < lo + HEAD_DIM)).astype(F32).astype(BF16)
         logits = jnp.dot(query * own_feat, key_t, preferred_element_type=F32)
         la = logits[:, :blk] + bias_ref[half * heads + h].astype(F32) + mask_a
-        lb = logits[:, blk:] + bias_in_ref[h].astype(F32) + mask_b
+        lb = logits[:, blk:] + bias_in_ref[half * heads + h].astype(F32) + mask_b
         peak = jnp.max(jnp.maximum(la, lb), axis=1, keepdims=True)
         probs = jnp.concatenate([jnp.exp(la - peak), jnp.exp(lb - peak)], axis=1).astype(BF16)
         value = jnp.concatenate([kv_t[hd + lo : hd + lo + HEAD_DIM], ones], axis=0).astype(BF16)
@@ -215,6 +215,7 @@
         out_specs=tuple([vmem] * len(outs)),
         scratch_shapes=list(scratch),
         cost_estimate=pl.CostEstimate(flops=flops, bytes_accessed=nbytes, transcendentals=trans),
+        compiler_params=pltpu.CompilerParams(vmem_limit_bytes=16 << 20),
     )(*args)
 
 
@@ -226,16 +227,14 @@
     width = w_out.shape[1]
     hd = D // 2
     half_heads = heads // 2
-    _, _, _, _, half = place()
     shape = jax.ShapeDtypeStruct
     swap_row = [(r * 4 + c, (1 - r) * 4 + (c ^ 1)) for r in range(2) for c in range(4)]
     swap_core = [(c, c ^ 1) for c in range(4)]
     swap_chip = [(c, c ^ 3) for c in range(4)]
 
-    gain = norm_gain.reshape(1, D)
+    gain = norm_gain
     single_in = lax.ppermute(single, ("row", "col"), swap_row)
-    bias_out = lax.dynamic_slice_in_dim(pair_bias, (1 - half) * half_heads, half_heads, 0)
-    bias_in = lax.ppermute(bias_out, "col", swap_core)
+    bias_in = lax.ppermute(pair_bias, "col", swap_core)
     query, gate, wkv, wo_own, wo_oth, res = call(
         prepare_kernel,
         [
@@ -246,7 +245,7 @@
             shape((width, hd), BF16),
             shape((width, n), F32),
         ],
-        (single, gain, w_query, query_bias.reshape(1, D), w_key, w_value, w_gate, w_out.T),
+        (single, gain, w_query, query_bias, w_key, w_value, w_gate, w_out.T),
         [pltpu.VMEM((D, D), F32)],
         flops=4 * n * D * D,
     )

time: 26.6 us -> 21.6 us (0.81)
  Pallas kernels: 11.1 us -> 3.78 us
  local copies, waits for them, and re-layouts: 4.4 us -> 7.72 us
  waiting for transfers between devices: 6.2 us -> 5.14 us
    pallas_call x4, Pallas kernels: 11.1 us -> 3.78 us  [call(): pl.pallas_call(kernel, out_shape=tuple(outs), in_specs=[vmem] * len(args)...]
    unnamed x14 -> x20, local copies, waits for them, and re-layouts: 2.13 us -> 7.72 us
    reshape x2 -> x0, local copies, waits for them, and re-layouts: 1.15 us -> none  [the longest x1 0.59 us: paired_plan(): gain = norm_gain.reshape(1, D)]
    dynamic_slice x1 -> x0, local copies, waits for them, and re-layouts: 1.12 us -> none  [paired_plan(): lax.dynamic_slice_in_dim(pair_bias, (1 - half) * half_heads, half_heads, 0)]
    ppermute x1, waiting for transfers between devices: 0.91 us -> 0.01 us  [paired_plan(): single_in = lax.ppermute(single, ('row', 'col'), swap_row)]
  transfers between devices with their start and end apart: 4 -> 4, of which waited for: 3 -> 2; matrix products, arithmetic and copies ran while one was open for 4% -> 0% of each run, Pallas kernels for 12% -> 5%
where the time goes in v2:
time: 21.6 us; the launch traced here: 21.2 us
  local copies, waits for them, and re-layouts  7.72 us (36%)
  waiting for transfers between devices  5.14 us (24%)
  starting transfers between devices  4.52 us (21%)
  Pallas kernels  3.78 us (18%)
    unnamed x20, local copies, waits for them, and re-layouts  7.72 us
    ppermute x1, waiting for transfers between devices, paired_plan(): recv = lax.ppermute(send, 'col', swap_chip)  3.95 us
    pallas_call x4, Pallas kernels, call(): pl.pallas_call(kernel, out_shape=tuple(outs), in_specs=[vmem] * len(args)...  3.78 us
    ppermute x1, starting transfers between devices, paired_plan(): single_in = lax.ppermute(single, ('row', 'col'), swap_row)  2.62 us
    ppermute x1, starting transfers between devices, paired_plan(): recv = lax.ppermute(send, 'col', swap_chip)  1.23 us
    ppermute x1, waiting for transfers between devices, paired_plan(): gated_oth = lax.ppermute(gated_own, 'col', swap_core)  1.19 us
    ppermute x1, starting transfers between devices, paired_plan(): bias_in = lax.ppermute(pair_bias, 'col', swap_core)  0.49 us
  transfers between devices with their start and end apart: 4, of which 2 were waited for; matrix products, arithmetic and copies ran while one was open for 0% of the time, Pallas kernels for 5%

profile of v2, /device:TPU:0, one launch (start us, length us, event | category | flops | bytes accessed | tf_op | source)
XLA Modules:
  0.0 21.2 jit_solution(18130075047336134796)
XLA Ops:
  0.0 0.0 copy-start
  0.0 0.5 %collective-permute-start.1 = (bf16[16,256,128]{2,1,0:T(8,128)(2,1)}, bf16[16,256,128]{2,1,0:T(8,128)(2,1)S(1)}, u32[]{:S(2)}, u32[]{:S(2)}) collective-permute-start(bf16[16,256,128]{2,1,0:T(8,128)(2,1)} %bias_ref.1), channel_id=1, source_target_pairs={{0,1},{1,0},{2,3},{3,2},{4,5},{5,4},{6,7},{7,6},{8,9},{9,8},{10,11... | collective-permute-start | bytes 3145736 | tf_op jit(solution)/shard_map/ppermute | solution.py:237
  0.5 2.6 %collective-permute-start = (bf16[256,384]{1,0:T(8,128)(2,1)}, bf16[256,384]{1,0:T(8,128)(2,1)S(1)}, u32[]{:S(2)}, u32[]{:S(2)}) collective-permute-start(bf16[256,384]{1,0:T(8,128)(2,1)} %own_ref.1), channel_id=1, source_target_pairs={{0,5},{1,4},{2,7},{3,6},{4,1},{5,0},{6,3},{7,2},{8,13},{9,12},{10,... | collective-permute-start | bytes 589832 | tf_op jit(solution)/shard_map/ppermute | solution.py:236
  3.1 1.0 %copy-done.1 = bf16[256,384]{1,0:T(8,128)(2,1)S(1)} copy-done((bf16[256,384]{1,0:T(8,128)(2,1)S(1)}, bf16[256,384]{1,0:T(8,128)(2,1)}, u32[]{:S(2)}) %copy-start.1) | copy-done | bytes 196632
  4.1 1.0 %copy-done.2 = bf16[384,384]{1,0:T(8,128)(2,1)S(1)} copy-done((bf16[384,384]{1,0:T(8,128)(2,1)S(1)}, bf16[384,384]{1,0:T(8,128)(2,1)}, u32[]{:S(2)}) %copy-start.2) | copy-done | bytes 294936
  5.0 1.0 %copy-done.3 = bf16[384,384]{1,0:T(8,128)(2,1)S(1)} copy-done((bf16[384,384]{1,0:T(8,128)(2,1)S(1)}, bf16[384,384]{1,0:T(8,128)(2,1)}, u32[]{:S(2)}) %copy-start.3) | copy-done | bytes 294936
  6.0 1.0 %copy-done.4 = bf16[384,384]{1,0:T(8,128)(2,1)S(1)} copy-done((bf16[384,384]{1,0:T(8,128)(2,1)S(1)}, bf16[384,384]{1,0:T(8,128)(2,1)}, u32[]{:S(2)}) %copy-start.4) | copy-done | bytes 294936
  7.0 1.0 %copy-done.5 = bf16[384,384]{1,0:T(8,128)(2,1)S(1)} copy-done((bf16[384,384]{1,0:T(8,128)(2,1)S(1)}, bf16[384,384]{1,0:T(8,128)(2,1)}, u32[]{:S(2)}) %copy-start.5) | copy-done | bytes 294936
  7.9 0.9 %copy-done.6 = bf16[384,96]{0,1:T(8,128)(2,1)S(1)} copy-done((bf16[384,96]{0,1:T(8,128)(2,1)S(1)}, bf16[384,96]{0,1:T(8,128)(2,1)}, u32[]{:S(2)}) %copy-start.6) | copy-done | bytes 73752
  8.8 0.7 %copy-done.7 = f32[384]{0:T(512)S(1)} copy-done((f32[384]{0:T(512)S(1)}, f32[384]{0:T(512)}, u32[]{:S(2)}) %copy-start.7) | copy-done | bytes 1560
  9.5 0.7 %copy-done.8 = f32[384]{0:T(512)S(1)} copy-done((f32[384]{0:T(512)S(1)}, f32[384]{0:T(512)}, u32[]{:S(2)}) %copy-start.8) | copy-done | bytes 1560
  10.2 1.0 %shard_map.100 = (bf16[256,192]{1,0:T(8,128)(2,1)S(1)}, f32[192,256]{1,0:T(8,128)S(1)}, bf16[384,384]{1,0:T(8,128)(2,1)S(1)}, bf16[96,192]{1,0:T(8,128)(2,1)S(1)...) custom-call(bf16[256,384]{1,0:T(8,128)(2,1)S(1)} %copy-done.1, f32[384]{0:T(512)S(1)} %copy-done.7, ...), custom_call_target="tpu_custom_call" | custom-call | flops 150994944 | bytes 2214912 | tf_op jit(solution)/shard_map/pallas_call | solution.py:211
  11.1 0.0 collective-permute-done.recv_ref
  11.1 0.0 collective-permute-done.1.bias_in_ref
  11.2 0.0 copy-start.9
  11.2 0.0 copy-done
  11.2 0.7 %copy-done.9 = s32[512]{0:T(512)S(1)} copy-done((s32[512]{0:T(512)S(1)}, s32[512]{0:T(512)}, u32[]{:S(2)}) %copy-start.9) | copy-done | bytes 2072
  11.8 1.9 %shard_map.101 = (bf16[216,256]{1,0:T(8,128)(2,1)S(1)}, f32[192,256]{1,0:T(8,128)S(1)}, f32[8,256]{1,0:T(8,128)S(1)}) custom-call(bf16[256,384]{1,0:T(8,128)(2,1)S(1)} %collective-permute-done.recv_ref, bf16[256,384]{1,0:T(8,128)(2,1)S(1)} %copy-done.1, f32[384]{0:T(512)S(1)} %copy-done.7, bf16[384,384]{1,0:T(8,128)(2,1)S(1)} %get-tuple-element.14.wkv_ref, ...), custom_call_target="tpu_custom_call" | custom-call | flops 150994944 | bytes 3202560 | tf_op jit(solution)/shard_map/pallas_call | solution.py:211
  13.8 1.2 %collective-permute-start.2 = (bf16[216,256]{1,0:T(8,128)(2,1)S(1)}, bf16[216,256]{1,0:T(8,128)(2,1)S(1)}, u32[]{:S(2)}, u32[]{:S(2)}) collective-permute-start(bf16[216,256]{1,0:T(8,128)(2,1)S(1)} %get-tuple-element.16), channel_id=1, source_target_pairs={{0,3},{1,2},{2,1},{3,0},{4,7},{5,6},{6,5},{7,4},{8,11},{9,10},{10,... | collective-permute-start | bytes 331784 | tf_op jit(solution)/shard_map/ppermute | solution.py:264
  15.0 4.0 %collective-permute-done.2.recv_ref = bf16[216,256]{1,0:T(8,128)(2,1)S(1)} collective-permute-done((bf16[216,256]{1,0:T(8,128)(2,1)S(1)}, bf16[216,256]{1,0:T(8,128)(2,1)S(1)}, u32[]{:S(2)}, u32[]{:S(2)}) %collective-permute-start.2) | collective-permute-done | bytes 110624 | tf_op jit(solution)/shard_map/ppermute | solution.py:264
  19.0 0.1 shard_map.102.own_ref
  19.0 0.2 collective-permute-start.3
  19.2 1.2 %collective-permute-done.3.oth_ref = bf16[192,256]{1,0:T(8,128)(2,1)S(1)} collective-permute-done((bf16[192,256]{1,0:T(8,128)(2,1)S(1)}, bf16[192,256]{1,0:T(8,128)(2,1)S(1)}, u32[]{:S(2)}, u32[]{:S(2)}) %collective-permute-start.3) | collective-permute-done | bytes 98336 | tf_op jit(solution)/shard_map/ppermute | solution.py:266
  20.4 0.8 %shard_map.103 = f32[96,256]{1,0:T(8,128)} custom-call(bf16[192,256]{1,0:T(8,128)(2,1)S(1)} %shard_map.102.own_ref, bf16[192,256]{1,0:T(8,128)(2,1)S(1)} %collective-permute-done.3.oth_ref, bf16[96,192]{1,0:T(8,128)(2,1)S(1)} %get-tuple-element.20.wo_own_ref, bf16[96,192]{1,0:T(8,128)(2,1)S(1)} %get-tuple-element.21.wo_oth_ref, ...), custom_call_target="tpu_custom_call" | custom-call | flops 18874368 | bytes 466944 | tf_op jit(solution)/shard_map/pallas_call | solution.py:211
  (8 shorter events, 0.0 us)
Async XLA Ops:
  0.0 11.2 %copy-start = (bf16[16,256,128]{2,1,0:T(8,128)(2,1)S(1)}, bf16[16,256,128]{2,1,0:T(8,128)(2,1)}, u32[]{:S(2)}) copy-start(bf16[16,256,128]{2,1,0:T(8,128)(2,1)} %bias_ref.1) | copy-start | bytes 3145732
  0.0 11.1 %collective-permute-start.1 = (bf16[16,256,128]{2,1,0:T(8,128)(2,1)}, bf16[16,256,128]{2,1,0:T(8,128)(2,1)S(1)}, u32[]{:S(2)}, u32[]{:S(2)}) collective-permute-start(bf16[16,256,128]{2,1,0:T(8,128)(2,1)} %bias_ref.1), channel_id=1, source_target_pairs={{0,1},{1,0},{2,3},{3,2},{4,5},{5,4},{6,7},{7,6},{8,9},{9,8},{10,11... | collective-permute-start | bytes 3145736 | tf_op jit(solution)/shard_map/ppermute | solution.py:237
  0.5 10.6 %collective-permute-start = (bf16[256,384]{1,0:T(8,128)(2,1)}, bf16[256,384]{1,0:T(8,128)(2,1)S(1)}, u32[]{:S(2)}, u32[]{:S(2)}) collective-permute-start(bf16[256,384]{1,0:T(8,128)(2,1)} %own_ref.1), channel_id=1, source_target_pairs={{0,5},{1,4},{2,7},{3,6},{4,1},{5,0},{6,3},{7,2},{8,13},{9,12},{10,... | collective-permute-start | bytes 589832 | tf_op jit(solution)/shard_map/ppermute | solution.py:236
  3.1 1.0 %copy-start.1 = (bf16[256,384]{1,0:T(8,128)(2,1)S(1)}, bf16[256,384]{1,0:T(8,128)(2,1)}, u32[]{:S(2)}) copy-start(bf16[256,384]{1,0:T(8,128)(2,1)} %own_ref.1) | copy-start | bytes 589828
  4.1 1.0 %copy-start.2 = (bf16[384,384]{1,0:T(8,128)(2,1)S(1)}, bf16[384,384]{1,0:T(8,128)(2,1)}, u32[]{:S(2)}) copy-start(bf16[384,384]{1,0:T(8,128)(2,1)} %wq_ref.1) | copy-start | bytes 884740
  5.0 1.0 %copy-start.3 = (bf16[384,384]{1,0:T(8,128)(2,1)S(1)}, bf16[384,384]{1,0:T(8,128)(2,1)}, u32[]{:S(2)}) copy-start(bf16[384,384]{1,0:T(8,128)(2,1)} %wk_ref.1) | copy-start | bytes 884740
  6.0 1.0 %copy-start.4 = (bf16[384,384]{1,0:T(8,128)(2,1)S(1)}, bf16[384,384]{1,0:T(8,128)(2,1)}, u32[]{:S(2)}) copy-start(bf16[384,384]{1,0:T(8,128)(2,1)} %wv_ref.1) | copy-start | bytes 884740
  7.0 1.0 %copy-start.5 = (bf16[384,384]{1,0:T(8,128)(2,1)S(1)}, bf16[384,384]{1,0:T(8,128)(2,1)}, u32[]{:S(2)}) copy-start(bf16[384,384]{1,0:T(8,128)(2,1)} %wg_ref.1) | copy-start | bytes 884740
  7.9 0.9 %copy-start.6 = (bf16[384,96]{0,1:T(8,128)(2,1)S(1)}, bf16[384,96]{0,1:T(8,128)(2,1)}, u32[]{:S(2)}) copy-start(bf16[384,96]{0,1:T(8,128)(2,1)} %param.19) | copy-start | bytes 221188
  8.8 0.7 %copy-start.7 = (f32[384]{0:T(512)S(1)}, f32[384]{0:T(512)}, u32[]{:S(2)}) copy-start(f32[384]{0:T(512)} %gain_ref.3) | copy-start | bytes 4612
  9.5 0.7 %copy-start.8 = (f32[384]{0:T(512)S(1)}, f32[384]{0:T(512)}, u32[]{:S(2)}) copy-start(f32[384]{0:T(512)} %bq_ref.1) | copy-start | bytes 4612
  11.2 0.7 %copy-start.9 = (s32[512]{0:T(512)S(1)}, s32[512]{0:T(512)}, u32[]{:S(2)}) copy-start(s32[512]{0:T(512)} %param.12) | copy-start | bytes 6148
  13.8 5.2 %collective-permute-start.2 = (bf16[216,256]{1,0:T(8,128)(2,1)S(1)}, bf16[216,256]{1,0:T(8,128)(2,1)S(1)}, u32[]{:S(2)}, u32[]{:S(2)}) collective-permute-start(bf16[216,256]{1,0:T(8,128)(2,1)S(1)} %get-tuple-element.16), channel_id=1, source_target_pairs={{0,3},{1,2},{2,1},{3,0},{4,7},{5,6},{6,5},{7,4},{8,11},{9,10},{10,... | collective-permute-start | bytes 331784 | tf_op jit(solution)/shard_map/ppermute | solution.py:264
  19.0 1.4 %collective-permute-start.3 = (bf16[192,256]{1,0:T(8,128)(2,1)S(1)}, bf16[192,256]{1,0:T(8,128)(2,1)S(1)}, u32[]{:S(2)}, u32[]{:S(2)}) collective-permute-start(bf16[192,256]{1,0:T(8,128)(2,1)S(1)} %shard_map.102.own_ref), channel_id=1, source_target_pairs={{0,1},{1,0},{2,3},{3,2},{4,5},{5,4},{6,7},{7,6},{8,9},{9,8},{10,11... | collective-permute-start | bytes 294920 | tf_op jit(solution)/shard_map/ppermute | solution.py:266

commit v3 on v2

--- a/solution.py
+++ b/solution.py
@@ -88,33 +88,58 @@
 
 
 def prepare_kernel(
-    single_ref, gain_ref, wq_ref, bq_ref, wk_ref, wv_ref, wg_ref, wo_ref,
-    q_ref, gate_ref, wkv_ref, wo_own_ref, wo_oth_ref, res_ref, tmp_ref,
+    single_hbm, gain_hbm, mask_hbm, wq_hbm, bq_hbm, wk_hbm, wv_hbm, wg_hbm, wo_hbm,
+    q_ref, gate_ref, wkv_ref, wo_own_ref, wo_oth_ref, res_ref, gain_out_ref, bar_ref,
+    single_ref, gain_ref, mask_ref, wq_ref, bq_ref, wk_ref, wv_ref, wg_ref, wo_ref, tmp_ref, sems,
 ):
-    _, col, _, _, half = place()
+    _, col, chip, core, half = place()
+    sources = (single_hbm, gain_hbm, wq_hbm, bq_hbm, wg_hbm, wk_hbm, wv_hbm, wo_hbm, mask_hbm)
+    targets = (single_ref, gain_ref, wq_ref, bq_ref, wg_ref, wk_ref, wv_ref, wo_ref, mask_ref)
+    copies = [
+        pltpu.make_async_copy(src, dst, sems.at[i])
+        for i, (src, dst) in enumerate(zip(sources, targets))
+    ]
+    for copy in copies:
+        copy.start()
     hd = D // 2
     width = wo_ref.shape[0]
+    n = single_ref.shape[0]
+    blk = n // 2
+    copies[0].wait()
+    copies[1].wait()
+    gain_out_ref[...] = gain_ref[...]
     x = single_ref[...].astype(F32)
+    tmp_ref[:, :n] = x.T
+    res_ref[...] = tmp_ref[pl.ds(pl.multiple_of(col * width, 8), width), :n]
     normed = layer_norm(single_ref[...], gain_ref[...][None, :])
+    copies[2].wait()
+    copies[3].wait()
     query = (jnp.dot(normed, wq_ref[...], preferred_element_type=F32) + bq_ref[...][None, :]) * SCALE
     q_ref[...] = jnp.where(half == 0, query[:, :hd], query[:, hd:]).astype(BF16)
-    n = x.shape[0]
+    copies[4].wait()
     gate = jnp.dot(normed, wg_ref[...], preferred_element_type=F32)
     tmp_ref[:, :n] = gate.T
     gate_ref[...] = jax.nn.sigmoid(tmp_ref[pl.ds(pl.multiple_of(half * hd, 8), hd), :n])
-    tmp_ref[:, :n] = x.T
-    res_ref[...] = tmp_ref[pl.ds(pl.multiple_of(col * width, 8), width), :n]
+    copies[5].wait()
     tmp_ref[...] = wk_ref[...].astype(F32).T
     wkv_ref[:hd, :] = tmp_ref[pl.ds(pl.multiple_of(half * hd, 8), hd), :].astype(BF16)
+    copies[6].wait()
     tmp_ref[...] = wv_ref[...].astype(F32).T
     wkv_ref[hd:, :] = tmp_ref[pl.ds(pl.multiple_of(half * hd, 8), hd), :].astype(BF16)
+    copies[7].wait()
     wo = wo_ref[...].astype(F32)
     wo_own_ref[...] = jnp.where(half == 0, wo[:, :hd], wo[:, hd:]).astype(BF16)
     wo_oth_ref[...] = jnp.where(half == 0, wo[:, hd:], wo[:, :hd]).astype(BF16)
+    copies[8].wait()
+    base = chip * n
+    first = pl.multiple_of(base + core * blk, blk)
+    second = pl.multiple_of(base + (1 - core) * blk, blk)
+    bar_ref[:, :blk] = (mask_ref[:, pl.ds(first, blk)].astype(F32) - 1.0) * 1000000.0
+    bar_ref[:, blk:] = (mask_ref[:, pl.ds(second, blk)].astype(F32) - 1.0) * 1000000.0
 
 
 def partial_kernel(
-    recv_ref, own_ref, gain_ref, wkv_ref, q_ref, bias_ref, bias_in_ref, mask_ref,
+    recv_ref, own_ref, gain_ref, wkv_ref, q_ref, bias_ref, bias_in_ref, bar_ref,
     send_ref, att_ref, lse_ref, kv_ref,
 ):
     row, _, chip, core, half = place()
@@ -136,11 +161,8 @@
         kv_ref[:blk, :] = recv_ref[pl.ds(first, blk), :]
         kv_ref[blk:, :] = recv_ref[pl.ds(second, blk), :]
 
-    base = chip * n_k
-    mask_a = mask_ref[:, pl.ds(pl.multiple_of(base + first, blk), blk)]
-    mask_b = mask_ref[:, pl.ds(pl.multiple_of(base + second, blk), blk)]
-    mask_a = (mask_a.astype(F32) - 1.0) * 1000000.0
-    mask_b = (mask_b.astype(F32) - 1.0) * 1000000.0
+    mask_a = bar_ref[:, :blk]
+    mask_b = bar_ref[:, blk:]
     normed = layer_norm(kv_ref[...], gain_ref[...][None, :])
     kv_t = lax.dot_general(wkv_ref[...], normed, NT, preferred_element_type=F32)
     key_t = kv_t[:hd].astype(BF16)
@@ -205,13 +227,16 @@
     )
 
 
-def call(kernel, outs, args, scratch=(), flops=0, trans=0):
+def call(kernel, outs, args, scratch=(), flops=0, trans=0, fetch=False):
     vmem = pl.BlockSpec(memory_space=pltpu.VMEM)
+    source = pl.BlockSpec(memory_space=pltpu.HBM) if fetch else vmem
+    if fetch:
+        args = [pltpu.with_memory_space_constraint(a, pltpu.HBM) for a in args]
     nbytes = sum(math.prod(a.shape) * a.dtype.itemsize for a in (*args, *outs))
     return pl.pallas_call(
         kernel,
         out_shape=tuple(outs),
-        in_specs=[vmem] * len(args),
+        in_specs=[source] * len(args),
         out_specs=tuple([vmem] * len(outs)),
         scratch_shapes=list(scratch),
         cost_estimate=pl.CostEstimate(flops=flops, bytes_accessed=nbytes, transcendentals=trans),
@@ -232,10 +257,12 @@
     swap_core = [(c, c ^ 1) for c in range(4)]
     swap_chip = [(c, c ^ 3) for c in range(4)]
 
-    gain = norm_gain
     single_in = lax.ppermute(single, ("row", "col"), swap_row)
     bias_in = lax.ppermute(pair_bias, "col", swap_core)
-    query, gate, wkv, wo_own, wo_oth, res = call(
+    fetched = (
+        single, norm_gain, token_mask.reshape(1, -1), w_query, query_bias, w_key, w_value, w_gate, w_out.T,
+    )
+    query, gate, wkv, wo_own, wo_oth, res, gain, bar = call(
         prepare_kernel,
         [
             shape((n, hd), BF16),
@@ -244,10 +271,17 @@
             shape((width, hd), BF16),
             shape((width, hd), BF16),
             shape((width, n), F32),
+            shape((D,), F32),
+            shape((1, n), F32),
         ],
-        (single, gain, w_query, query_bias, w_key, w_value, w_gate, w_out.T),
-        [pltpu.VMEM((D, D), F32)],
+        fetched,
+        [
+            *(pltpu.VMEM(a.shape, a.dtype) for a in fetched),
+            pltpu.VMEM((D, D), F32),
+            pltpu.SemaphoreType.DMA((len(fetched),)),
+        ],
         flops=4 * n * D * D,
+        fetch=True,
     )
     send, att, lse = call(
         partial_kernel,
@@ -256,7 +290,7 @@
             shape((hd, n), F32),
             shape((half_heads, n), F32),
         ],
-        (single_in, single, gain, wkv, query, pair_bias, bias_in, token_mask.reshape(1, -1)),
+        (single_in, single, gain, wkv, query, pair_bias, bias_in, bar),
         [pltpu.VMEM((n, D), BF16)],
         flops=4 * n * D * D,
         trans=half_heads * n * n,

time: 21.6 us -> 18 us (0.83); the launches traced: 21.2 us -> 17.9 us
  local copies, waits for them, and re-layouts: 7.72 us -> 0.01 us
  waiting for transfers between devices: 5.14 us -> 7.45 us
  Pallas kernels: 3.78 us -> 5.72 us
    unnamed x20 -> x4, local copies, waits for them, and re-layouts: 7.72 us -> 0.01 us
    ppermute x1, waiting for transfers between devices: 0.01 us -> 2.54 us  [paired_plan(): single_in = lax.ppermute(single, ('row', 'col'), swap_row)]
    pallas_call x4, Pallas kernels: 3.78 us -> 5.72 us  [call(): pl.pallas_call(kernel, out_shape=tuple(outs), in_specs=[source] * len(arg...]
    ppermute x1, waiting for transfers between devices: 3.95 us -> 3.73 us  [paired_plan(): recv = lax.ppermute(send, 'col', swap_chip)]
  transfers between devices with their start and end apart: 4 -> 4, of which waited for: 2 -> 3; matrix products, arithmetic and copies ran while one was open for 0% -> 0% of each run, Pallas kernels for 5% -> 16%
where the time goes in v3:
time: 18 us; the launch traced here: 17.9 us
  waiting for transfers between devices  7.45 us (41%)
  Pallas kernels  5.72 us (32%)
  starting transfers between devices  4.69 us (26%)
    pallas_call x4, Pallas kernels, call(): pl.pallas_call(kernel, out_shape=tuple(outs), in_specs=[source] * len(arg...  5.72 us
    ppermute x1, waiting for transfers between devices, paired_plan(): recv = lax.ppermute(send, 'col', swap_chip)  3.73 us
    ppermute x1, starting transfers between devices, paired_plan(): single_in = lax.ppermute(single, ('row', 'col'), swap_row)  2.62 us
    ppermute x1, waiting for transfers between devices, paired_plan(): single_in = lax.ppermute(single, ('row', 'col'), swap_row)  2.54 us
    ppermute x1, starting transfers between devices, paired_plan(): recv = lax.ppermute(send, 'col', swap_chip)  1.4 us
    ppermute x1, waiting for transfers between devices, paired_plan(): gated_oth = lax.ppermute(gated_own, 'col', swap_core)  1.18 us
    ppermute x1, starting transfers between devices, paired_plan(): bias_in = lax.ppermute(pair_bias, 'col', swap_core)  0.49 us
  transfers between devices with their start and end apart: 4, of which 3 were waited for; matrix products, arithmetic and copies ran while one was open for 0% of the time, Pallas kernels for 16%

profile of v3, /device:TPU:0, one launch (start us, length us, event | category | flops | bytes accessed | tf_op | source)
XLA Modules:
  0.0 17.9 jit_solution(15797033275300626255)
XLA Ops:
  0.0 0.0 copy-start
  0.0 0.5 %collective-permute-start.1 = (bf16[16,256,128]{2,1,0:T(8,128)(2,1)}, bf16[16,256,128]{2,1,0:T(8,128)(2,1)S(1)}, u32[]{:S(2)}, u32[]{:S(2)}) collective-permute-start(bf16[16,256,128]{2,1,0:T(8,128)(2,1)} %bias_ref.1), channel_id=1, source_target_pairs={{0,1},{1,0},{2,3},{3,2},{4,5},{5,4},{6,7},{7,6},{8,9},{9,8},{10,11... | collective-permute-start | bytes 3145736 | tf_op jit(solution)/shard_map/ppermute | solution.py:261
  0.5 2.6 %collective-permute-start = (bf16[256,384]{1,0:T(8,128)(2,1)}, bf16[256,384]{1,0:T(8,128)(2,1)S(1)}, u32[]{:S(2)}, u32[]{:S(2)}) collective-permute-start(bf16[256,384]{1,0:T(8,128)(2,1)} %own_ref.1), channel_id=1, source_target_pairs={{0,5},{1,4},{2,7},{3,6},{4,1},{5,0},{6,3},{7,2},{8,13},{9,12},{10,... | collective-permute-start | bytes 589832 | tf_op jit(solution)/shard_map/ppermute | solution.py:260
  3.1 0.0 copy-start.1
  3.1 2.9 %shard_map.100 = (bf16[256,192]{1,0:T(8,128)(2,1)S(1)}, f32[192,256]{1,0:T(8,128)S(1)}, bf16[384,384]{1,0:T(8,128)(2,1)S(1)}, bf16[96,192]{1,0:T(8,128)(2,1)S(1)...) custom-call(bf16[256,384]{1,0:T(8,128)(2,1)} %own_ref.1, ...), custom_call_target="tpu_custom_call" | custom-call | flops 150994944 | bytes 2219520 | tf_op jit(solution)/shard_map/pallas_call | solution.py:236
  6.0 2.5 %collective-permute-done.recv_ref = bf16[256,384]{1,0:T(8,128)(2,1)S(1)} collective-permute-done((bf16[256,384]{1,0:T(8,128)(2,1)}, bf16[256,384]{1,0:T(8,128)(2,1)S(1)}, u32[]{:S(2)}, u32[]{:S(2)}) %collective-permute-start) | collective-permute-done | bytes 196640 | tf_op jit(solution)/shard_map/ppermute | solution.py:260
  8.5 0.0 collective-permute-done.1.bias_in_ref
  8.5 0.0 copy-done
  8.5 0.0 copy-done.1
  8.5 2.0 %shard_map.101 = (bf16[216,256]{1,0:T(8,128)(2,1)S(1)}, f32[192,256]{1,0:T(8,128)S(1)}, f32[8,256]{1,0:T(8,128)S(1)}) custom-call(bf16[256,384]{1,0:T(8,128)(2,1)S(1)} %collective-permute-done.recv_ref, bf16[256,384]{1,0:T(8,128)(2,1)S(1)} %copy-done.1, f32[384]{0:T(512)S(1)} %get-tuple-element.16.gain_ref, bf16[384,384]{1,0:T(8,128)(2,1)S(1)} %get-tuple-element.17.wkv_ref, ...), custom_call_target="tpu_custom_call" | custom-call | flops 150994944 | bytes 3201536 | tf_op jit(solution)/shard_map/pallas_call | solution.py:236
  10.5 1.4 %collective-permute-start.2 = (bf16[216,256]{1,0:T(8,128)(2,1)S(1)}, bf16[216,256]{1,0:T(8,128)(2,1)S(1)}, u32[]{:S(2)}, u32[]{:S(2)}) collective-permute-start(bf16[216,256]{1,0:T(8,128)(2,1)S(1)} %get-tuple-element.20), channel_id=1, source_target_pairs={{0,3},{1,2},{2,1},{3,0},{4,7},{5,6},{6,5},{7,4},{8,11},{9,10},{10,... | collective-permute-start | bytes 331784 | tf_op jit(solution)/shard_map/ppermute | solution.py:298
  11.9 3.7 %collective-permute-done.2.recv_ref = bf16[216,256]{1,0:T(8,128)(2,1)S(1)} collective-permute-done((bf16[216,256]{1,0:T(8,128)(2,1)S(1)}, bf16[216,256]{1,0:T(8,128)(2,1)S(1)}, u32[]{:S(2)}, u32[]{:S(2)}) %collective-permute-start.2) | collective-permute-done | bytes 110624 | tf_op jit(solution)/shard_map/ppermute | solution.py:298
  15.7 0.1 shard_map.102.own_ref
  15.7 0.2 %collective-permute-start.3 = (bf16[192,256]{1,0:T(8,128)(2,1)S(1)}, bf16[192,256]{1,0:T(8,128)(2,1)S(1)}, u32[]{:S(2)}, u32[]{:S(2)}) collective-permute-start(bf16[192,256]{1,0:T(8,128)(2,1)S(1)} %shard_map.102.own_ref), channel_id=1, source_target_pairs={{0,1},{1,0},{2,3},{3,2},{4,5},{5,4},{6,7},{7,6},{8,9},{9,8},{10,11... | collective-permute-start | bytes 294920 | tf_op jit(solution)/shard_map/ppermute | solution.py:300
  15.9 1.2 %collective-permute-done.3.oth_ref = bf16[192,256]{1,0:T(8,128)(2,1)S(1)} collective-permute-done((bf16[192,256]{1,0:T(8,128)(2,1)S(1)}, bf16[192,256]{1,0:T(8,128)(2,1)S(1)}, u32[]{:S(2)}, u32[]{:S(2)}) %collective-permute-start.3) | collective-permute-done | bytes 98336 | tf_op jit(solution)/shard_map/ppermute | solution.py:300
  17.1 0.8 %shard_map.103 = f32[96,256]{1,0:T(8,128)} custom-call(bf16[192,256]{1,0:T(8,128)(2,1)S(1)} %shard_map.102.own_ref, bf16[192,256]{1,0:T(8,128)(2,1)S(1)} %collective-permute-done.3.oth_ref, bf16[96,192]{1,0:T(8,128)(2,1)S(1)} %get-tuple-element.24.wo_own_ref, bf16[96,192]{1,0:T(8,128)(2,1)S(1)} %get-tuple-element.25.wo_oth_ref, ...), custom_call_target="tpu_custom_call" | custom-call | flops 18874368 | bytes 466944 | tf_op jit(solution)/shard_map/pallas_call | solution.py:236
Async XLA Ops:
  0.0 8.5 %copy-start = (bf16[16,256,128]{2,1,0:T(8,128)(2,1)S(1)}, bf16[16,256,128]{2,1,0:T(8,128)(2,1)}, u32[]{:S(2)}) copy-start(bf16[16,256,128]{2,1,0:T(8,128)(2,1)} %bias_ref.1) | copy-start | bytes 3145732
  0.0 8.5 %collective-permute-start.1 = (bf16[16,256,128]{2,1,0:T(8,128)(2,1)}, bf16[16,256,128]{2,1,0:T(8,128)(2,1)S(1)}, u32[]{:S(2)}, u32[]{:S(2)}) collective-permute-start(bf16[16,256,128]{2,1,0:T(8,128)(2,1)} %bias_ref.1), channel_id=1, source_target_pairs={{0,1},{1,0},{2,3},{3,2},{4,5},{5,4},{6,7},{7,6},{8,9},{9,8},{10,11... | collective-permute-start | bytes 3145736 | tf_op jit(solution)/shard_map/ppermute | solution.py:261
  0.5 8.0 %collective-permute-start = (bf16[256,384]{1,0:T(8,128)(2,1)}, bf16[256,384]{1,0:T(8,128)(2,1)S(1)}, u32[]{:S(2)}, u32[]{:S(2)}) collective-permute-start(bf16[256,384]{1,0:T(8,128)(2,1)} %own_ref.1), channel_id=1, source_target_pairs={{0,5},{1,4},{2,7},{3,6},{4,1},{5,0},{6,3},{7,2},{8,13},{9,12},{10,... | collective-permute-start | bytes 589832 | tf_op jit(solution)/shard_map/ppermute | solution.py:260
  3.1 5.4 %copy-start.1 = (bf16[256,384]{1,0:T(8,128)(2,1)S(1)}, bf16[256,384]{1,0:T(8,128)(2,1)}, u32[]{:S(2)}) copy-start(bf16[256,384]{1,0:T(8,128)(2,1)} %own_ref.1) | copy-start | bytes 589828
  10.5 5.1 %collective-permute-start.2 = (bf16[216,256]{1,0:T(8,128)(2,1)S(1)}, bf16[216,256]{1,0:T(8,128)(2,1)S(1)}, u32[]{:S(2)}, u32[]{:S(2)}) collective-permute-start(bf16[216,256]{1,0:T(8,128)(2,1)S(1)} %get-tuple-element.20), channel_id=1, source_target_pairs={{0,3},{1,2},{2,1},{3,0},{4,7},{5,6},{6,5},{7,4},{8,11},{9,10},{10,... | collective-permute-start | bytes 331784 | tf_op jit(solution)/shard_map/ppermute | solution.py:298
  15.7 1.4 %collective-permute-start.3 = (bf16[192,256]{1,0:T(8,128)(2,1)S(1)}, bf16[192,256]{1,0:T(8,128)(2,1)S(1)}, u32[]{:S(2)}, u32[]{:S(2)}) collective-permute-start(bf16[192,256]{1,0:T(8,128)(2,1)S(1)} %shard_map.102.own_ref), channel_id=1, source_target_pairs={{0,1},{1,0},{2,3},{3,2},{4,5},{5,4},{6,7},{7,6},{8,9},{9,8},{10,11... | collective-permute-start | bytes 294920 | tf_op jit(solution)/shard_map/ppermute | solution.py:300

commit v4 on v3

--- a/solution.py
+++ b/solution.py
@@ -1,4 +1,3 @@
-import functools
 import math
 
 import jax
@@ -16,6 +15,11 @@
 NT = (((1,), (1,)), ((), ()))
 F32 = jnp.float32
 BF16 = jnp.bfloat16
+PAD = 16
+AHEAD = 8
+CHUNK = 256
+BAR_HI = -999424.0
+BAR_LO = -576.0
 
 
 def layer_norm(single, norm_gain):
@@ -115,7 +119,14 @@
     copies[2].wait()
     copies[3].wait()
     query = (jnp.dot(normed, wq_ref[...], preferred_element_type=F32) + bq_ref[...][None, :]) * SCALE
-    q_ref[...] = jnp.where(half == 0, query[:, :hd], query[:, hd:]).astype(BF16)
+    query = jnp.where(half == 0, query[:, :hd], query[:, hd:])
+    query = jnp.concatenate([query, jnp.ones((n, PAD), F32)], axis=1)
+    feature = lax.broadcasted_iota(jnp.int32, query.shape, 1)
+    bar_rows = (feature == hd) | (feature == hd + 1)
+    for h in range(q_ref.shape[0]):
+        lo = h * HEAD_DIM
+        kept = ((feature >= lo) & (feature < lo + HEAD_DIM)) | bar_rows
+        q_ref[h] = jnp.where(kept, query, 0.0).astype(BF16)
     copies[4].wait()
     gate = jnp.dot(normed, wg_ref[...], preferred_element_type=F32)
     tmp_ref[:, :n] = gate.T
@@ -134,59 +145,67 @@
     base = chip * n
     first = pl.multiple_of(base + core * blk, blk)
     second = pl.multiple_of(base + (1 - core) * blk, blk)
-    bar_ref[:, :blk] = (mask_ref[:, pl.ds(first, blk)].astype(F32) - 1.0) * 1000000.0
-    bar_ref[:, blk:] = (mask_ref[:, pl.ds(second, blk)].astype(F32) - 1.0) * 1000000.0
+    masked = jnp.concatenate([mask_ref[:, pl.ds(first, blk)], mask_ref[:, pl.ds(second, blk)]], axis=1)
+    masked = 1.0 - masked.astype(F32)
+    pad_row = lax.broadcasted_iota(jnp.int32, (PAD, n), 0)
+    level = jnp.where(pad_row == 0, BAR_HI, jnp.where(pad_row == 1, BAR_LO, 0.0))
+    bar_ref[...] = (level * masked).astype(BF16)
 
 
 def partial_kernel(
     recv_ref, own_ref, gain_ref, wkv_ref, q_ref, bias_ref, bias_in_ref, bar_ref,
-    send_ref, att_ref, lse_ref, kv_ref,
+    send_ref, att_ref, lse_ref,
 ):
     row, _, chip, core, half = place()
     hd = D // 2
     heads = HEADS // 2
-    n_q = q_ref.shape[0]
+    n_q = q_ref.shape[1]
     n_k = recv_ref.shape[0]
     blk = n_k // 2
     first = pl.multiple_of(core * blk, blk)
     second = pl.multiple_of((1 - core) * blk, blk)
 
-    @pl.when(chip == row)
-    def _():
-        kv_ref[:blk, :] = own_ref[pl.ds(first, blk), :]
-        kv_ref[blk:, :] = own_ref[pl.ds(second, blk), :]
-
-    @pl.when(chip != row)
-    def _():
-        kv_ref[:blk, :] = recv_ref[pl.ds(first, blk), :]
-        kv_ref[blk:, :] = recv_ref[pl.ds(second, blk), :]
-
-    mask_a = bar_ref[:, :blk]
-    mask_b = bar_ref[:, blk:]
-    normed = layer_norm(kv_ref[...], gain_ref[...][None, :])
+    local = chip == row
+    block_a = jnp.where(local, own_ref[pl.ds(first, blk), :], recv_ref[pl.ds(first, blk), :])
+    block_b = jnp.where(local, own_ref[pl.ds(second, blk), :], recv_ref[pl.ds(second, blk), :])
+    tokens = jnp.concatenate([block_a, block_b], axis=0)
+    normed = layer_norm(tokens, gain_ref[...][None, :])
     kv_t = lax.dot_general(wkv_ref[...], normed, NT, preferred_element_type=F32)
-    key_t = kv_t[:hd].astype(BF16)
-    query = q_ref[...]
-    feature = lax.broadcasted_iota(jnp.int32, (1, hd), 1)
+    key_t = jnp.concatenate([kv_t[:hd].astype(BF16), bar_ref[...]], axis=0)
     lane = lax.broadcasted_iota(jnp.int32, (n_q, 128), 1)
     peaks = jnp.zeros((n_q, 128), F32)
     ones = jnp.ones((8, n_k), F32)
     sums = []
-    for h in range(heads):
+
+    def logits_of(task):
+        h, start = task
+        return jnp.dot(q_ref[h, start : start + CHUNK, :], key_t, preferred_element_type=F32)
+
+    tasks = [(h, start) for h in range(heads) for start in range(0, n_q, CHUNK)]
+    ready = [logits_of(task) for task in tasks[:AHEAD]]
+    probs, tops = [], []
+    for i, (h, start) in enumerate(tasks):
         lo = h * HEAD_DIM
-        own_feat = ((feature >= lo) & (feature < lo + HEAD_DIM)).astype(F32).astype(BF16)
-        logits = jnp.dot(query * own_feat, key_t, preferred_element_type=F32)
-        la = logits[:, :blk] + bias_ref[half * heads + h].astype(F32) + mask_a
-        lb = logits[:, blk:] + bias_in_ref[half * heads + h].astype(F32) + mask_b
+        rows = slice(start, start + CHUNK)
+        logits = ready.pop(0)
+        if i + AHEAD < len(tasks):
+            ready.append(logits_of(tasks[i + AHEAD]))
+        la = logits[:, :blk] + bias_ref[half * heads + h, rows, :].astype(F32)
+        lb = logits[:, blk:] + bias_in_ref[half * heads + h, rows, :].astype(F32)
         peak = jnp.max(jnp.maximum(la, lb), axis=1, keepdims=True)
-        probs = jnp.concatenate([jnp.exp(la - peak), jnp.exp(lb - peak)], axis=1).astype(BF16)
+        probs.append(jnp.concatenate([jnp.exp(la - peak), jnp.exp(lb - peak)], axis=1).astype(BF16))
+        tops.append(peak)
+        if start + CHUNK < n_q:
+            continue
         value = jnp.concatenate([kv_t[hd + lo : hd + lo + HEAD_DIM], ones], axis=0).astype(BF16)
-        out = lax.dot_general(value, probs, NT, preferred_element_type=F32)
+        out = lax.dot_general(
+            value, jnp.concatenate(probs, axis=0), NT, preferred_element_type=F32
+        )
         total = out[HEAD_DIM : HEAD_DIM + 1]
-        att = out[:HEAD_DIM] / total
-        att_ref[lo : lo + HEAD_DIM, :] = att
+        att_ref[lo : lo + HEAD_DIM, :] = out[:HEAD_DIM] / total
         sums.append(total)
-        peaks = jnp.where(lane == h, peak, peaks)
+        peaks = jnp.where(lane == h, jnp.concatenate(tops, axis=0), peaks)
+        probs, tops = [], []
     lse = peaks.T[:heads] + jnp.log(jnp.concatenate(sums, axis=0))
     lse_ref[...] = lse
     hi = lse.astype(BF16)
@@ -248,7 +267,7 @@
     single, pair_bias, token_mask, norm_gain, w_query, query_bias, w_key, w_value, w_gate, w_out
 ):
     n = single.shape[0]
-    heads, rows, cols = pair_bias.shape
+    heads, _, _ = pair_bias.shape
     width = w_out.shape[1]
     hd = D // 2
     half_heads = heads // 2
@@ -265,14 +284,14 @@
     query, gate, wkv, wo_own, wo_oth, res, gain, bar = call(
         prepare_kernel,
         [
-            shape((n, hd), BF16),
+            shape((half_heads, n, hd + PAD), BF16),
             shape((hd, n), F32),
             shape((D, D), BF16),
             shape((width, hd), BF16),
             shape((width, hd), BF16),
             shape((width, n), F32),
             shape((D,), F32),
-            shape((1, n), F32),
+            shape((PAD, n), BF16),
         ],
         fetched,
         [
@@ -291,7 +310,6 @@
             shape((half_heads, n), F32),
         ],
         (single_in, single, gain, wkv, query, pair_bias, bias_in, bar),
-        [pltpu.VMEM((n, D), BF16)],
         flops=4 * n * D * D,
         trans=half_heads * n * n,
     )

time: 18 us -> 17.6 us (0.978)
  Pallas kernels: 5.72 us -> 5.3 us
    pallas_call x4, Pallas kernels: 5.72 us -> 5.3 us  [call(): pl.pallas_call(kernel, out_shape=tuple(outs), in_specs=[source] * len(arg...]
  transfers between devices with their start and end apart: 4 -> 4, of which waited for: 3 -> 3; matrix products, arithmetic and copies ran while one was open for 0% -> 0% of each run, Pallas kernels for 16% -> 17%
where the time goes in v4:
time: 17.6 us; the launch traced here: 17.4 us
  waiting for transfers between devices  7.39 us (42%)
  Pallas kernels  5.3 us (30%)
  starting transfers between devices  4.69 us (27%)
    pallas_call x4, Pallas kernels, call(): pl.pallas_call(kernel, out_shape=tuple(outs), in_specs=[source] * len(arg...  5.3 us
    ppermute x1, waiting for transfers between devices, paired_plan(): recv = lax.ppermute(send, 'col', swap_chip)  3.73 us
    ppermute x1, starting transfers between devices, paired_plan(): single_in = lax.ppermute(single, ('row', 'col'), swap_row)  2.62 us
    ppermute x1, waiting for transfers between devices, paired_plan(): single_in = lax.ppermute(single, ('row', 'col'), swap_row)  2.47 us
    ppermute x1, starting transfers between devices, paired_plan(): recv = lax.ppermute(send, 'col', swap_chip)  1.4 us
    ppermute x1, waiting for transfers between devices, paired_plan(): gated_oth = lax.ppermute(gated_own, 'col', swap_core)  1.18 us
    ppermute x1, starting transfers between devices, paired_plan(): bias_in = lax.ppermute(pair_bias, 'col', swap_core)  0.49 us
  transfers between devices with their start and end apart: 4, of which 3 were waited for; matrix products, arithmetic and copies ran while one was open for 0% of the time, Pallas kernels for 17%

profile of v4, /device:TPU:0, one launch (start us, length us, event | category | flops | bytes accessed | tf_op | source)
XLA Modules:
  0.0 17.4 jit_solution(894761429041361620)
XLA Ops:
  0.0 0.0 copy-start
  0.0 0.5 %collective-permute-start.1 = (bf16[16,256,128]{2,1,0:T(8,128)(2,1)}, bf16[16,256,128]{2,1,0:T(8,128)(2,1)S(1)}, u32[]{:S(2)}, u32[]{:S(2)}) collective-permute-start(bf16[16,256,128]{2,1,0:T(8,128)(2,1)} %bias_ref.1), channel_id=1, source_target_pairs={{0,1},{1,0},{2,3},{3,2},{4,5},{5,4},{6,7},{7,6},{8,9},{9,8},{10,11... | collective-permute-start | bytes 3145736 | tf_op jit(solution)/shard_map/ppermute | solution.py:280
  0.5 2.6 %collective-permute-start = (bf16[256,384]{1,0:T(8,128)(2,1)}, bf16[256,384]{1,0:T(8,128)(2,1)S(1)}, u32[]{:S(2)}, u32[]{:S(2)}) collective-permute-start(bf16[256,384]{1,0:T(8,128)(2,1)} %own_ref.1), channel_id=1, source_target_pairs={{0,5},{1,4},{2,7},{3,6},{4,1},{5,0},{6,3},{7,2},{8,13},{9,12},{10,... | collective-permute-start | bytes 589832 | tf_op jit(solution)/shard_map/ppermute | solution.py:279
  3.1 0.0 copy-start.1
  3.1 2.9 %shard_map.100 = (bf16[8,256,208]{2,1,0:T(8,128)(2,1)S(1)}, f32[192,256]{1,0:T(8,128)S(1)}, bf16[384,384]{1,0:T(8,128)(2,1)S(1)}, bf16[96,192]{1,0:T(8,128)(2,1)...) custom-call(bf16[256,384]{1,0:T(8,128)(2,1)} %own_ref.1, ...), custom_call_target="tpu_custom_call" | custom-call | flops 150994944 | bytes 2980352 | tf_op jit(solution)/shard_map/pallas_call | solution.py:255
  6.1 2.5 %collective-permute-done.recv_ref = bf16[256,384]{1,0:T(8,128)(2,1)S(1)} collective-permute-done((bf16[256,384]{1,0:T(8,128)(2,1)}, bf16[256,384]{1,0:T(8,128)(2,1)S(1)}, u32[]{:S(2)}, u32[]{:S(2)}) %collective-permute-start) | collective-permute-done | bytes 196640 | tf_op jit(solution)/shard_map/ppermute | solution.py:279
  8.5 0.0 collective-permute-done.1.bias_in_ref
  8.5 0.0 copy-done
  8.5 0.0 copy-done.1
  8.5 1.5 %shard_map.101 = (bf16[216,256]{1,0:T(8,128)(2,1)S(1)}, f32[192,256]{1,0:T(8,128)S(1)}, f32[8,256]{1,0:T(8,128)S(1)}) custom-call(bf16[256,384]{1,0:T(8,128)(2,1)S(1)} %collective-permute-done.recv_ref, bf16[256,384]{1,0:T(8,128)(2,1)S(1)} %copy-done.1, f32[384]{0:T(512)S(1)} %get-tuple-element.16.gain_ref, bf16[384,384]{1,0:T(8,128)(2,1)S(1)} %get-tuple-element.17.wkv_ref, ...), custom_call_target="tpu_custom_call" | custom-call | flops 150994944 | bytes 3962368 | tf_op jit(solution)/shard_map/pallas_call | solution.py:255
  10.0 1.4 %collective-permute-start.2 = (bf16[216,256]{1,0:T(8,128)(2,1)S(1)}, bf16[216,256]{1,0:T(8,128)(2,1)S(1)}, u32[]{:S(2)}, u32[]{:S(2)}) collective-permute-start(bf16[216,256]{1,0:T(8,128)(2,1)S(1)} %get-tuple-element.20), channel_id=1, source_target_pairs={{0,3},{1,2},{2,1},{3,0},{4,7},{5,6},{6,5},{7,4},{8,11},{9,10},{10,... | collective-permute-start | bytes 331784 | tf_op jit(solution)/shard_map/ppermute | solution.py:316
  11.4 3.7 %collective-permute-done.2.recv_ref = bf16[216,256]{1,0:T(8,128)(2,1)S(1)} collective-permute-done((bf16[216,256]{1,0:T(8,128)(2,1)S(1)}, bf16[216,256]{1,0:T(8,128)(2,1)S(1)}, u32[]{:S(2)}, u32[]{:S(2)}) %collective-permute-start.2) | collective-permute-done | bytes 110624 | tf_op jit(solution)/shard_map/ppermute | solution.py:316
  15.2 0.1 shard_map.102.own_ref
  15.2 0.2 %collective-permute-start.3 = (bf16[192,256]{1,0:T(8,128)(2,1)S(1)}, bf16[192,256]{1,0:T(8,128)(2,1)S(1)}, u32[]{:S(2)}, u32[]{:S(2)}) collective-permute-start(bf16[192,256]{1,0:T(8,128)(2,1)S(1)} %shard_map.102.own_ref), channel_id=1, source_target_pairs={{0,1},{1,0},{2,3},{3,2},{4,5},{5,4},{6,7},{7,6},{8,9},{9,8},{10,11... | collective-permute-start | bytes 294920 | tf_op jit(solution)/shard_map/ppermute | solution.py:318
  15.4 1.2 %collective-permute-done.3.oth_ref = bf16[192,256]{1,0:T(8,128)(2,1)S(1)} collective-permute-done((bf16[192,256]{1,0:T(8,128)(2,1)S(1)}, bf16[192,256]{1,0:T(8,128)(2,1)S(1)}, u32[]{:S(2)}, u32[]{:S(2)}) %collective-permute-start.3) | collective-permute-done | bytes 98336 | tf_op jit(solution)/shard_map/ppermute | solution.py:318
  16.6 0.8 %shard_map.103 = f32[96,256]{1,0:T(8,128)} custom-call(bf16[192,256]{1,0:T(8,128)(2,1)S(1)} %shard_map.102.own_ref, bf16[192,256]{1,0:T(8,128)(2,1)S(1)} %collective-permute-done.3.oth_ref, bf16[96,192]{1,0:T(8,128)(2,1)S(1)} %get-tuple-element.24.wo_own_ref, bf16[96,192]{1,0:T(8,128)(2,1)S(1)} %get-tuple-element.25.wo_oth_ref, ...), custom_call_target="tpu_custom_call" | custom-call | flops 18874368 | bytes 466944 | tf_op jit(solution)/shard_map/pallas_call | solution.py:255
Async XLA Ops:
  0.0 8.5 %copy-start = (bf16[16,256,128]{2,1,0:T(8,128)(2,1)S(1)}, bf16[16,256,128]{2,1,0:T(8,128)(2,1)}, u32[]{:S(2)}) copy-start(bf16[16,256,128]{2,1,0:T(8,128)(2,1)} %bias_ref.1) | copy-start | bytes 3145732
  0.0 8.5 %collective-permute-start.1 = (bf16[16,256,128]{2,1,0:T(8,128)(2,1)}, bf16[16,256,128]{2,1,0:T(8,128)(2,1)S(1)}, u32[]{:S(2)}, u32[]{:S(2)}) collective-permute-start(bf16[16,256,128]{2,1,0:T(8,128)(2,1)} %bias_ref.1), channel_id=1, source_target_pairs={{0,1},{1,0},{2,3},{3,2},{4,5},{5,4},{6,7},{7,6},{8,9},{9,8},{10,11... | collective-permute-start | bytes 3145736 | tf_op jit(solution)/shard_map/ppermute | solution.py:280
  0.5 8.0 %collective-permute-start = (bf16[256,384]{1,0:T(8,128)(2,1)}, bf16[256,384]{1,0:T(8,128)(2,1)S(1)}, u32[]{:S(2)}, u32[]{:S(2)}) collective-permute-start(bf16[256,384]{1,0:T(8,128)(2,1)} %own_ref.1), channel_id=1, source_target_pairs={{0,5},{1,4},{2,7},{3,6},{4,1},{5,0},{6,3},{7,2},{8,13},{9,12},{10,... | collective-permute-start | bytes 589832 | tf_op jit(solution)/shard_map/ppermute | solution.py:279
  3.1 5.4 %copy-start.1 = (bf16[256,384]{1,0:T(8,128)(2,1)S(1)}, bf16[256,384]{1,0:T(8,128)(2,1)}, u32[]{:S(2)}) copy-start(bf16[256,384]{1,0:T(8,128)(2,1)} %own_ref.1) | copy-start | bytes 589828
  10.0 5.1 %collective-permute-start.2 = (bf16[216,256]{1,0:T(8,128)(2,1)S(1)}, bf16[216,256]{1,0:T(8,128)(2,1)S(1)}, u32[]{:S(2)}, u32[]{:S(2)}) collective-permute-start(bf16[216,256]{1,0:T(8,128)(2,1)S(1)} %get-tuple-element.20), channel_id=1, source_target_pairs={{0,3},{1,2},{2,1},{3,0},{4,7},{5,6},{6,5},{7,4},{8,11},{9,10},{10,... | collective-permute-start | bytes 331784 | tf_op jit(solution)/shard_map/ppermute | solution.py:316
  15.2 1.4 %collective-permute-start.3 = (bf16[192,256]{1,0:T(8,128)(2,1)S(1)}, bf16[192,256]{1,0:T(8,128)(2,1)S(1)}, u32[]{:S(2)}, u32[]{:S(2)}) collective-permute-start(bf16[192,256]{1,0:T(8,128)(2,1)S(1)} %shard_map.102.own_ref), channel_id=1, source_target_pairs={{0,1},{1,0},{2,3},{3,2},{4,5},{5,4},{6,7},{7,6},{8,9},{9,8},{10,11... | collective-permute-start | bytes 294920 | tf_op jit(solution)/shard_map/ppermute | solution.py:318

commit v5 on v4

--- a/solution.py
+++ b/solution.py
@@ -89,6 +89,15 @@
     core = col % 2
     half = (chip + core) % 2
     return row, col, chip, core, half
+
+
+def pick_kernel(single_hbm, out_ref, sem):
+    _, _, _, core, _ = place()
+    blk = out_ref.shape[0]
+    start = pl.multiple_of((1 - core) * blk, blk)
+    copy = pltpu.make_async_copy(single_hbm.at[pl.ds(start, blk), :], out_ref, sem)
+    copy.start()
+    copy.wait()
 
 
 def prepare_kernel(
@@ -153,21 +162,21 @@
 
 
 def partial_kernel(
-    recv_ref, own_ref, gain_ref, wkv_ref, q_ref, bias_ref, bias_in_ref, bar_ref,
+    recv_ref, other_ref, own_ref, gain_ref, wkv_ref, q_ref, bias_ref, bias_in_ref, bar_ref,
     send_ref, att_ref, lse_ref,
 ):
     row, _, chip, core, half = place()
     hd = D // 2
     heads = HEADS // 2
     n_q = q_ref.shape[1]
-    n_k = recv_ref.shape[0]
+    n_k = own_ref.shape[0]
     blk = n_k // 2
     first = pl.multiple_of(core * blk, blk)
     second = pl.multiple_of((1 - core) * blk, blk)
 
     local = chip == row
-    block_a = jnp.where(local, own_ref[pl.ds(first, blk), :], recv_ref[pl.ds(first, blk), :])
-    block_b = jnp.where(local, own_ref[pl.ds(second, blk), :], recv_ref[pl.ds(second, blk), :])
+    block_a = jnp.where(local, own_ref[pl.ds(first, blk), :], recv_ref[...])
+    block_b = jnp.where(local, own_ref[pl.ds(second, blk), :], other_ref[...])
     tokens = jnp.concatenate([block_a, block_b], axis=0)
     normed = layer_norm(tokens, gain_ref[...][None, :])
     kv_t = lax.dot_general(wkv_ref[...], normed, NT, preferred_element_type=F32)
@@ -276,11 +285,14 @@
     swap_core = [(c, c ^ 1) for c in range(4)]
     swap_chip = [(c, c ^ 3) for c in range(4)]
 
-    single_in = lax.ppermute(single, ("row", "col"), swap_row)
+    dma = pltpu.SemaphoreType.DMA(())
+    (picked,) = call(pick_kernel, [shape((n // 2, D), BF16)], (single,), [dma], fetch=True)
+    rows_in = lax.ppermute(picked, ("row", "col"), swap_row)
     bias_in = lax.ppermute(pair_bias, "col", swap_core)
     fetched = (
         single, norm_gain, token_mask.reshape(1, -1), w_query, query_bias, w_key, w_value, w_gate, w_out.T,
     )
+    rows_other = lax.ppermute(rows_in, "col", swap_core)
     query, gate, wkv, wo_own, wo_oth, res, gain, bar = call(
         prepare_kernel,
         [
@@ -309,7 +321,7 @@
             shape((hd, n), F32),
             shape((half_heads, n), F32),
         ],
-        (single_in, single, gain, wkv, query, pair_bias, bias_in, bar),
+        (rows_in, rows_other, single, gain, wkv, query, pair_bias, bias_in, bar),
         flops=4 * n * D * D,
         trans=half_heads * n * n,
     )

time: 17.6 us -> 19 us (1.080)
  Pallas kernels: 5.3 us -> 6.15 us
  starting transfers between devices: 4.69 us -> 5.24 us
    pallas_call x4 -> x5, Pallas kernels: 5.3 us -> 6.15 us  [call(): pl.pallas_call(kernel, out_shape=tuple(outs), in_specs=[source] * len(arg...]
    ppermute x1 -> x2, waiting for transfers between devices: 2.47 us -> 3.08 us  [the longest x1 3.08 us: paired_plan(): rows_in = lax.ppermute(picked, ('row', 'col'), swap_row)]
    ppermute x1, waiting for transfers between devices: 3.73 us -> 3.36 us  [paired_plan(): recv = lax.ppermute(send, 'col', swap_chip)]
    ppermute x1, starting transfers between devices: 0.18 us -> 0.5 us  [paired_plan(): gated_oth = lax.ppermute(gated_own, 'col', swap_core)]
    ppermute x1, waiting for transfers between devices: 1.18 us -> 0.94 us  [paired_plan(): gated_oth = lax.ppermute(gated_own, 'col', swap_core)]
    ppermute x1 -> x2, starting transfers between devices: 2.62 us -> 2.8 us  [the longest x1 2.68 us: paired_plan(): rows_in = lax.ppermute(picked, ('row', 'col'), swap_row)]
  transfers between devices with their start and end apart: 4 -> 5, of which waited for: 3 -> 3; matrix products, arithmetic and copies ran while one was open for 0% -> 0% of each run, Pallas kernels for 17% -> 20%
where the time goes in v5:
time: 19 us; the launch traced here: 18.9 us
  waiting for transfers between devices  7.38 us (39%)
  Pallas kernels  6.15 us (32%)
  starting transfers between devices  5.24 us (28%)
    pallas_call x5, Pallas kernels, call(): pl.pallas_call(kernel, out_shape=tuple(outs), in_specs=[source] * len(arg...  6.15 us
    ppermute x1, waiting for transfers between devices, paired_plan(): recv = lax.ppermute(send, 'col', swap_chip)  3.36 us
    ppermute x1, waiting for transfers between devices, paired_plan(): rows_in = lax.ppermute(picked, ('row', 'col'), swap_row)  3.08 us
    ppermute x1, starting transfers between devices, paired_plan(): rows_in = lax.ppermute(picked, ('row', 'col'), swap_row)  2.68 us
    ppermute x1, starting transfers between devices, paired_plan(): recv = lax.ppermute(send, 'col', swap_chip)  1.45 us
    ppermute x1, waiting for transfers between devices, paired_plan(): gated_oth = lax.ppermute(gated_own, 'col', swap_core)  0.94 us
    ppermute x1, starting transfers between devices, paired_plan(): gated_oth = lax.ppermute(gated_own, 'col', swap_core)  0.5 us
    ppermute x1, starting transfers between devices, paired_plan(): bias_in = lax.ppermute(pair_bias, 'col', swap_core)  0.49 us
  transfers between devices with their start and end apart: 5, of which 3 were waited for; matrix products, arithmetic and copies ran while one was open for 0% of the time, Pallas kernels for 20%

profile of v5, /device:TPU:0, one launch (start us, length us, event | category | flops | bytes accessed | tf_op | source)
XLA Modules:
  0.0 18.9 jit_solution(14961515196520697218)
XLA Ops:
  0.0 0.0 copy-start.1
  0.0 0.5 %collective-permute-start.2 = (bf16[16,256,128]{2,1,0:T(8,128)(2,1)}, bf16[16,256,128]{2,1,0:T(8,128)(2,1)S(1)}, u32[]{:S(2)}, u32[]{:S(2)}) collective-permute-start(bf16[16,256,128]{2,1,0:T(8,128)(2,1)} %bias_ref.1), channel_id=1, source_target_pairs={{0,1},{1,0},{2,3},{3,2},{4,5},{5,4},{6,7},{7,6},{8,9},{9,8},{10,11... | collective-permute-start | bytes 3145736 | tf_op jit(solution)/shard_map/ppermute | solution.py:291
  0.5 0.9 %shard_map.100 = bf16[128,384]{1,0:T(8,128)(2,1)S(1)} custom-call(bf16[256,384]{1,0:T(8,128)(2,1)} %own_ref.1), custom_call_target="tpu_custom_call" | custom-call | bytes 294912 | tf_op jit(solution)/shard_map/pallas_call | solution.py:264
  1.4 2.7 %collective-permute-start = (bf16[128,384]{1,0:T(8,128)(2,1)S(1)}, bf16[128,384]{1,0:T(8,128)(2,1)S(1)}, u32[]{:S(2)}, u32[]{:S(2)}) collective-permute-start(bf16[128,384]{1,0:T(8,128)(2,1)S(1)} %shard_map.100), channel_id=1, source_target_pairs={{0,5},{1,4},{2,7},{3,6},{4,1},{5,0},{6,3},{7,2},{8,13},{9,12},{10,... | collective-permute-start | bytes 294920 | tf_op jit(solution)/shard_map/ppermute | solution.py:290
  4.1 3.1 %collective-permute-done.recv_ref = bf16[128,384]{1,0:T(8,128)(2,1)S(1)} collective-permute-done((bf16[128,384]{1,0:T(8,128)(2,1)S(1)}, bf16[128,384]{1,0:T(8,128)(2,1)S(1)}, u32[]{:S(2)}, u32[]{:S(2)}) %collective-permute-start) | collective-permute-done | bytes 98336 | tf_op jit(solution)/shard_map/ppermute | solution.py:290
  7.2 0.1 collective-permute-start.1
  7.3 0.0 copy-start
  7.3 2.9 %shard_map.101 = (bf16[8,256,208]{2,1,0:T(8,128)(2,1)S(1)}, f32[192,256]{1,0:T(8,128)S(1)}, bf16[384,384]{1,0:T(8,128)(2,1)S(1)}, bf16[96,192]{1,0:T(8,128)(2,1)...) custom-call(bf16[256,384]{1,0:T(8,128)(2,1)} %own_ref.1, ...), custom_call_target="tpu_custom_call" | custom-call | flops 150994944 | bytes 2980352 | tf_op jit(solution)/shard_map/pallas_call | solution.py:264
  10.2 0.0 collective-permute-done.1.other_ref
  10.2 0.0 collective-permute-done.2.bias_in_ref
  10.2 0.0 copy-done.1
  10.2 0.0 copy-done
  10.2 1.5 %shard_map.102 = (bf16[216,256]{1,0:T(8,128)(2,1)S(1)}, f32[192,256]{1,0:T(8,128)S(1)}, f32[8,256]{1,0:T(8,128)S(1)}) custom-call(bf16[128,384]{1,0:T(8,128)(2,1)S(1)} %collective-permute-done.recv_ref, bf16[128,384]{1,0:T(8,128)(2,1)S(1)} %collective-permute-done.1.other_ref, bf16[256,384]{1,0:T(8,128)(2,1)S(1)} %copy-done, ...), custom_call_target="tpu_custom_call" | custom-call | flops 150994944 | bytes 3962368 | tf_op jit(solution)/shard_map/pallas_call | solution.py:264
  11.7 1.4 %collective-permute-start.3 = (bf16[216,256]{1,0:T(8,128)(2,1)S(1)}, bf16[216,256]{1,0:T(8,128)(2,1)S(1)}, u32[]{:S(2)}, u32[]{:S(2)}) collective-permute-start(bf16[216,256]{1,0:T(8,128)(2,1)S(1)} %get-tuple-element.20), channel_id=1, source_target_pairs={{0,3},{1,2},{2,1},{3,0},{4,7},{5,6},{6,5},{7,4},{8,11},{9,10},{10,... | collective-permute-start | bytes 331784 | tf_op jit(solution)/shard_map/ppermute | solution.py:328
  13.2 3.4 %collective-permute-done.3.recv_ref = bf16[216,256]{1,0:T(8,128)(2,1)S(1)} collective-permute-done((bf16[216,256]{1,0:T(8,128)(2,1)S(1)}, bf16[216,256]{1,0:T(8,128)(2,1)S(1)}, u32[]{:S(2)}, u32[]{:S(2)}) %collective-permute-start.3) | collective-permute-done | bytes 110624 | tf_op jit(solution)/shard_map/ppermute | solution.py:328
  16.5 0.1 shard_map.103.own_ref
  16.6 0.5 %collective-permute-start.4 = (bf16[192,256]{1,0:T(8,128)(2,1)S(1)}, bf16[192,256]{1,0:T(8,128)(2,1)S(1)}, u32[]{:S(2)}, u32[]{:S(2)}) collective-permute-start(bf16[192,256]{1,0:T(8,128)(2,1)S(1)} %shard_map.103.own_ref), channel_id=1, source_target_pairs={{0,1},{1,0},{2,3},{3,2},{4,5},{5,4},{6,7},{7,6},{8,9},{9,8},{10,11... | collective-permute-start | bytes 294920 | tf_op jit(solution)/shard_map/ppermute | solution.py:330
  17.1 0.9 %collective-permute-done.4.oth_ref = bf16[192,256]{1,0:T(8,128)(2,1)S(1)} collective-permute-done((bf16[192,256]{1,0:T(8,128)(2,1)S(1)}, bf16[192,256]{1,0:T(8,128)(2,1)S(1)}, u32[]{:S(2)}, u32[]{:S(2)}) %collective-permute-start.4) | collective-permute-done | bytes 98336 | tf_op jit(solution)/shard_map/ppermute | solution.py:330
  18.0 0.8 %shard_map.104 = f32[96,256]{1,0:T(8,128)} custom-call(bf16[192,256]{1,0:T(8,128)(2,1)S(1)} %shard_map.103.own_ref, bf16[192,256]{1,0:T(8,128)(2,1)S(1)} %collective-permute-done.4.oth_ref, bf16[96,192]{1,0:T(8,128)(2,1)S(1)} %get-tuple-element.24.wo_own_ref, bf16[96,192]{1,0:T(8,128)(2,1)S(1)} %get-tuple-element.25.wo_oth_ref, ...), custom_call_target="tpu_custom_call" | custom-call | flops 18874368 | bytes 466944 | tf_op jit(solution)/shard_map/pallas_call | solution.py:264
Async XLA Ops:
  0.0 10.2 %copy-start.1 = (bf16[16,256,128]{2,1,0:T(8,128)(2,1)S(1)}, bf16[16,256,128]{2,1,0:T(8,128)(2,1)}, u32[]{:S(2)}) copy-start(bf16[16,256,128]{2,1,0:T(8,128)(2,1)} %bias_ref.1) | copy-start | bytes 3145732
  0.0 10.2 %collective-permute-start.2 = (bf16[16,256,128]{2,1,0:T(8,128)(2,1)}, bf16[16,256,128]{2,1,0:T(8,128)(2,1)S(1)}, u32[]{:S(2)}, u32[]{:S(2)}) collective-permute-start(bf16[16,256,128]{2,1,0:T(8,128)(2,1)} %bias_ref.1), channel_id=1, source_target_pairs={{0,1},{1,0},{2,3},{3,2},{4,5},{5,4},{6,7},{7,6},{8,9},{9,8},{10,11... | collective-permute-start | bytes 3145736 | tf_op jit(solution)/shard_map/ppermute | solution.py:291
  1.4 5.8 %collective-permute-start = (bf16[128,384]{1,0:T(8,128)(2,1)S(1)}, bf16[128,384]{1,0:T(8,128)(2,1)S(1)}, u32[]{:S(2)}, u32[]{:S(2)}) collective-permute-start(bf16[128,384]{1,0:T(8,128)(2,1)S(1)} %shard_map.100), channel_id=1, source_target_pairs={{0,5},{1,4},{2,7},{3,6},{4,1},{5,0},{6,3},{7,2},{8,13},{9,12},{10,... | collective-permute-start | bytes 294920 | tf_op jit(solution)/shard_map/ppermute | solution.py:290
  7.2 3.0 %collective-permute-start.1 = (bf16[128,384]{1,0:T(8,128)(2,1)S(1)}, bf16[128,384]{1,0:T(8,128)(2,1)S(1)}, u32[]{:S(2)}, u32[]{:S(2)}) collective-permute-start(bf16[128,384]{1,0:T(8,128)(2,1)S(1)} %collective-permute-done.recv_ref), channel_id=1, source_target_pairs={{0,1},{1,0},{2,3},{3,2},{4,5},{5,4},{6,7},{7,6},{8,9},{9,8},{10,11... | collective-permute-start | bytes 294920 | tf_op jit(solution)/shard_map/ppermute | solution.py:295
  7.3 2.9 %copy-start = (bf16[256,384]{1,0:T(8,128)(2,1)S(1)}, bf16[256,384]{1,0:T(8,128)(2,1)}, u32[]{:S(2)}) copy-start(bf16[256,384]{1,0:T(8,128)(2,1)} %own_ref.1) | copy-start | bytes 589828
  11.7 4.8 %collective-permute-start.3 = (bf16[216,256]{1,0:T(8,128)(2,1)S(1)}, bf16[216,256]{1,0:T(8,128)(2,1)S(1)}, u32[]{:S(2)}, u32[]{:S(2)}) collective-permute-start(bf16[216,256]{1,0:T(8,128)(2,1)S(1)} %get-tuple-element.20), channel_id=1, source_target_pairs={{0,3},{1,2},{2,1},{3,0},{4,7},{5,6},{6,5},{7,4},{8,11},{9,10},{10,... | collective-permute-start | bytes 331784 | tf_op jit(solution)/shard_map/ppermute | solution.py:328
  16.6 1.4 %collective-permute-start.4 = (bf16[192,256]{1,0:T(8,128)(2,1)S(1)}, bf16[192,256]{1,0:T(8,128)(2,1)S(1)}, u32[]{:S(2)}, u32[]{:S(2)}) collective-permute-start(bf16[192,256]{1,0:T(8,128)(2,1)S(1)} %shard_map.103.own_ref), channel_id=1, source_target_pairs={{0,1},{1,0},{2,3},{3,2},{4,5},{5,4},{6,7},{7,6},{8,9},{9,8},{10,11... | collective-permute-start | bytes 294920 | tf_op jit(solution)/shard_map/ppermute | solution.py:330

commit v6 on v4

--- a/solution.py
+++ b/solution.py
@@ -152,11 +152,19 @@
     bar_ref[...] = (level * masked).astype(BF16)
 
 
+def widen_kernel(own_ref, other_ref, out_ref):
+    _, _, _, _, half = place()
+    heads, _, n_k = out_ref.shape
+    for h in range(heads):
+        out_ref[h, :, : n_k // 2] = own_ref[half * heads + h].astype(F32)
+        out_ref[h, :, n_k // 2 :] = other_ref[half * heads + h].astype(F32)
+
+
 def partial_kernel(
-    recv_ref, own_ref, gain_ref, wkv_ref, q_ref, bias_ref, bias_in_ref, bar_ref,
+    recv_ref, own_ref, gain_ref, wkv_ref, q_ref, bias_ref, bar_ref,
     send_ref, att_ref, lse_ref,
 ):
-    row, _, chip, core, half = place()
+    row, _, chip, core, _ = place()
     hd = D // 2
     heads = HEADS // 2
     n_q = q_ref.shape[1]
@@ -168,10 +176,12 @@
     local = chip == row
     block_a = jnp.where(local, own_ref[pl.ds(first, blk), :], recv_ref[pl.ds(first, blk), :])
     block_b = jnp.where(local, own_ref[pl.ds(second, blk), :], recv_ref[pl.ds(second, blk), :])
+    gain = gain_ref[...][None, :]
     tokens = jnp.concatenate([block_a, block_b], axis=0)
-    normed = layer_norm(tokens, gain_ref[...][None, :])
-    kv_t = lax.dot_general(wkv_ref[...], normed, NT, preferred_element_type=F32)
-    key_t = jnp.concatenate([kv_t[:hd].astype(BF16), bar_ref[...]], axis=0)
+    normed = layer_norm(tokens, gain)
+    k_t = lax.dot_general(wkv_ref[:hd, :], normed, NT, preferred_element_type=F32)
+    v_t = lax.dot_general(wkv_ref[hd:, :], normed, NT, preferred_element_type=F32)
+    key_t = jnp.concatenate([k_t.astype(BF16), bar_ref[...]], axis=0)
     lane = lax.broadcasted_iota(jnp.int32, (n_q, 128), 1)
     peaks = jnp.zeros((n_q, 128), F32)
     ones = jnp.ones((8, n_k), F32)
@@ -190,19 +200,21 @@
         logits = ready.pop(0)
         if i + AHEAD < len(tasks):
             ready.append(logits_of(tasks[i + AHEAD]))
-        la = logits[:, :blk] + bias_ref[half * heads + h, rows, :].astype(F32)
-        lb = logits[:, blk:] + bias_in_ref[half * heads + h, rows, :].astype(F32)
+        la = logits[:, :blk] + bias_ref[h, rows, :blk]
+        lb = logits[:, blk:] + bias_ref[h, rows, blk:]
         peak = jnp.max(jnp.maximum(la, lb), axis=1, keepdims=True)
         probs.append(jnp.concatenate([jnp.exp(la - peak), jnp.exp(lb - peak)], axis=1).astype(BF16))
         tops.append(peak)
         if start + CHUNK < n_q:
             continue
-        value = jnp.concatenate([kv_t[hd + lo : hd + lo + HEAD_DIM], ones], axis=0).astype(BF16)
+        value = jnp.concatenate([v_t[lo : lo + HEAD_DIM], ones], axis=0).astype(BF16)
         out = lax.dot_general(
             value, jnp.concatenate(probs, axis=0), NT, preferred_element_type=F32
         )
         total = out[HEAD_DIM : HEAD_DIM + 1]
-        att_ref[lo : lo + HEAD_DIM, :] = out[:HEAD_DIM] / total
+        att = out[:HEAD_DIM] / total
+        att_ref[lo : lo + HEAD_DIM, :] = att
+        send_ref[lo : lo + HEAD_DIM, :] = att.astype(BF16)
         sums.append(total)
         peaks = jnp.where(lane == h, jnp.concatenate(tops, axis=0), peaks)
         probs, tops = [], []
@@ -212,7 +224,6 @@
     rest = lse - hi.astype(F32)
     mid = rest.astype(BF16)
     low = (rest - mid.astype(F32)).astype(BF16)
-    send_ref[:hd, :] = att_ref[...].astype(BF16)
     send_ref[hd : hd + heads, :] = hi
     send_ref[hd + heads : hd + 2 * heads, :] = mid
     send_ref[hd + 2 * heads :, :] = low
@@ -302,6 +313,9 @@
         flops=4 * n * D * D,
         fetch=True,
     )
+    (bias,) = call(
+        widen_kernel, [shape((half_heads, n, n), F32)], (pair_bias, bias_in), flops=half_heads * n * n
+    )
     send, att, lse = call(
         partial_kernel,
         [
@@ -309,7 +323,7 @@
             shape((hd, n), F32),
             shape((half_heads, n), F32),
         ],
-        (single_in, single, gain, wkv, query, pair_bias, bias_in, bar),
+        (single_in, single, gain, wkv, query, bias, bar),
         flops=4 * n * D * D,
         trans=half_heads * n * n,
     )

time: 17.6 us -> 17.3 us (0.983)
    pallas_call x4 -> x5, Pallas kernels: 5.3 us -> 5.19 us  [call(): pl.pallas_call(kernel, out_shape=tuple(outs), in_specs=[source] * len(arg...]
  transfers between devices with their start and end apart: 4 -> 4, of which waited for: 3 -> 3; matrix products, arithmetic and copies ran while one was open for 0% -> 0% of each run, Pallas kernels for 17% -> 18%
where the time goes in v6:
time: 17.3 us; the launch traced here: 17.2 us
  waiting for transfers between devices  7.25 us (42%)
  Pallas kernels  5.19 us (30%)
  starting transfers between devices  4.7 us (27%)
    pallas_call x5, Pallas kernels, call(): pl.pallas_call(kernel, out_shape=tuple(outs), in_specs=[source] * len(arg...  5.19 us
    ppermute x1, waiting for transfers between devices, paired_plan(): recv = lax.ppermute(send, 'col', swap_chip)  3.72 us
    ppermute x1, starting transfers between devices, paired_plan(): single_in = lax.ppermute(single, ('row', 'col'), swap_row)  2.62 us
    ppermute x1, waiting for transfers between devices, paired_plan(): single_in = lax.ppermute(single, ('row', 'col'), swap_row)  2.35 us
    ppermute x1, starting transfers between devices, paired_plan(): recv = lax.ppermute(send, 'col', swap_chip)  1.41 us
    ppermute x1, waiting for transfers between devices, paired_plan(): gated_oth = lax.ppermute(gated_own, 'col', swap_core)  1.18 us
    ppermute x1, starting transfers between devices, paired_plan(): bias_in = lax.ppermute(pair_bias, 'col', swap_core)  0.49 us
  transfers between devices with their start and end apart: 4, of which 3 were waited for; matrix products, arithmetic and copies ran while one was open for 0% of the time, Pallas kernels for 18%

profile of v6, /device:TPU:0, one launch (start us, length us, event | category | flops | bytes accessed | tf_op | source)
XLA Modules:
  0.0 17.2 jit_solution(12774254991281867474)
XLA Ops:
  0.0 0.0 copy-start
  0.0 0.5 %collective-permute-start.1 = (bf16[16,256,128]{2,1,0:T(8,128)(2,1)}, bf16[16,256,128]{2,1,0:T(8,128)(2,1)S(1)}, u32[]{:S(2)}, u32[]{:S(2)}) collective-permute-start(bf16[16,256,128]{2,1,0:T(8,128)(2,1)} %own_ref.2), channel_id=1, source_target_pairs={{0,1},{1,0},{2,3},{3,2},{4,5},{5,4},{6,7},{7,6},{8,9},{9,8},{10,11... | collective-permute-start | bytes 3145736 | tf_op jit(solution)/shard_map/ppermute | solution.py:291
  0.5 2.6 %collective-permute-start = (bf16[256,384]{1,0:T(8,128)(2,1)}, bf16[256,384]{1,0:T(8,128)(2,1)S(1)}, u32[]{:S(2)}, u32[]{:S(2)}) collective-permute-start(bf16[256,384]{1,0:T(8,128)(2,1)} %own_ref.3), channel_id=1, source_target_pairs={{0,5},{1,4},{2,7},{3,6},{4,1},{5,0},{6,3},{7,2},{8,13},{9,12},{10,... | collective-permute-start | bytes 589832 | tf_op jit(solution)/shard_map/ppermute | solution.py:290
  3.1 2.9 %shard_map.100 = (bf16[8,256,208]{2,1,0:T(8,128)(2,1)S(1)}, f32[192,256]{1,0:T(8,128)S(1)}, bf16[384,384]{1,0:T(8,128)(2,1)S(1)}, bf16[96,192]{1,0:T(8,128)(2,1)...) custom-call(bf16[256,384]{1,0:T(8,128)(2,1)} %own_ref.3, ...), custom_call_target="tpu_custom_call" | custom-call | flops 150994944 | bytes 2980352 | tf_op jit(solution)/shard_map/pallas_call | solution.py:266
  6.0 0.0 copy-start.1
  6.0 0.0 collective-permute-done.1.other_ref
  6.0 0.0 copy-done
  6.0 0.2 shard_map.101.bias_ref
  6.2 2.3 %collective-permute-done.recv_ref = bf16[256,384]{1,0:T(8,128)(2,1)S(1)} collective-permute-done((bf16[256,384]{1,0:T(8,128)(2,1)}, bf16[256,384]{1,0:T(8,128)(2,1)S(1)}, u32[]{:S(2)}, u32[]{:S(2)}) %collective-permute-start) | collective-permute-done | bytes 196640 | tf_op jit(solution)/shard_map/ppermute | solution.py:290
  8.5 0.0 copy-done.1
  8.5 1.3 %shard_map.102 = (bf16[216,256]{1,0:T(8,128)(2,1)S(1)}, f32[192,256]{1,0:T(8,128)S(1)}, f32[8,256]{1,0:T(8,128)S(1)}) custom-call(bf16[256,384]{1,0:T(8,128)(2,1)S(1)} %collective-permute-done.recv_ref, bf16[256,384]{1,0:T(8,128)(2,1)S(1)} %copy-done.1, f32[384]{0:T(512)S(1)} %get-tuple-element.16.gain_ref, bf16[384,384]{1,0:T(8,128)(2,1)S(1)} %get-tuple-element.17.wkv_ref, ...), custom_call_target="tpu_custom_call" | custom-call | flops 150994944 | bytes 3962368 | tf_op jit(solution)/shard_map/pallas_call | solution.py:266
  9.8 1.4 %collective-permute-start.2 = (bf16[216,256]{1,0:T(8,128)(2,1)S(1)}, bf16[216,256]{1,0:T(8,128)(2,1)S(1)}, u32[]{:S(2)}, u32[]{:S(2)}) collective-permute-start(bf16[216,256]{1,0:T(8,128)(2,1)S(1)} %get-tuple-element.20), channel_id=1, source_target_pairs={{0,3},{1,2},{2,1},{3,0},{4,7},{5,6},{6,5},{7,4},{8,11},{9,10},{10,... | collective-permute-start | bytes 331784 | tf_op jit(solution)/shard_map/ppermute | solution.py:330
  11.2 3.7 %collective-permute-done.2.recv_ref = bf16[216,256]{1,0:T(8,128)(2,1)S(1)} collective-permute-done((bf16[216,256]{1,0:T(8,128)(2,1)S(1)}, bf16[216,256]{1,0:T(8,128)(2,1)S(1)}, u32[]{:S(2)}, u32[]{:S(2)}) %collective-permute-start.2) | collective-permute-done | bytes 110624 | tf_op jit(solution)/shard_map/ppermute | solution.py:330
  15.0 0.1 shard_map.103.own_ref
  15.0 0.2 %collective-permute-start.3 = (bf16[192,256]{1,0:T(8,128)(2,1)S(1)}, bf16[192,256]{1,0:T(8,128)(2,1)S(1)}, u32[]{:S(2)}, u32[]{:S(2)}) collective-permute-start(bf16[192,256]{1,0:T(8,128)(2,1)S(1)} %shard_map.103.own_ref), channel_id=1, source_target_pairs={{0,1},{1,0},{2,3},{3,2},{4,5},{5,4},{6,7},{7,6},{8,9},{9,8},{10,11... | collective-permute-start | bytes 294920 | tf_op jit(solution)/shard_map/ppermute | solution.py:332
  15.2 1.2 %collective-permute-done.3.oth_ref = bf16[192,256]{1,0:T(8,128)(2,1)S(1)} collective-permute-done((bf16[192,256]{1,0:T(8,128)(2,1)S(1)}, bf16[192,256]{1,0:T(8,128)(2,1)S(1)}, u32[]{:S(2)}, u32[]{:S(2)}) %collective-permute-start.3) | collective-permute-done | bytes 98336 | tf_op jit(solution)/shard_map/ppermute | solution.py:332
  16.4 0.8 %shard_map.104 = f32[96,256]{1,0:T(8,128)} custom-call(bf16[192,256]{1,0:T(8,128)(2,1)S(1)} %shard_map.103.own_ref, bf16[192,256]{1,0:T(8,128)(2,1)S(1)} %collective-permute-done.3.oth_ref, bf16[96,192]{1,0:T(8,128)(2,1)S(1)} %get-tuple-element.24.wo_own_ref, bf16[96,192]{1,0:T(8,128)(2,1)S(1)} %get-tuple-element.25.wo_oth_ref, ...), custom_call_target="tpu_custom_call" | custom-call | flops 18874368 | bytes 466944 | tf_op jit(solution)/shard_map/pallas_call | solution.py:266
Async XLA Ops:
  0.0 6.0 %copy-start = (bf16[16,256,128]{2,1,0:T(8,128)(2,1)S(1)}, bf16[16,256,128]{2,1,0:T(8,128)(2,1)}, u32[]{:S(2)}) copy-start(bf16[16,256,128]{2,1,0:T(8,128)(2,1)} %own_ref.2) | copy-start | bytes 3145732
  0.0 6.0 %collective-permute-start.1 = (bf16[16,256,128]{2,1,0:T(8,128)(2,1)}, bf16[16,256,128]{2,1,0:T(8,128)(2,1)S(1)}, u32[]{:S(2)}, u32[]{:S(2)}) collective-permute-start(bf16[16,256,128]{2,1,0:T(8,128)(2,1)} %own_ref.2), channel_id=1, source_target_pairs={{0,1},{1,0},{2,3},{3,2},{4,5},{5,4},{6,7},{7,6},{8,9},{9,8},{10,11... | collective-permute-start | bytes 3145736 | tf_op jit(solution)/shard_map/ppermute | solution.py:291
  0.5 8.0 %collective-permute-start = (bf16[256,384]{1,0:T(8,128)(2,1)}, bf16[256,384]{1,0:T(8,128)(2,1)S(1)}, u32[]{:S(2)}, u32[]{:S(2)}) collective-permute-start(bf16[256,384]{1,0:T(8,128)(2,1)} %own_ref.3), channel_id=1, source_target_pairs={{0,5},{1,4},{2,7},{3,6},{4,1},{5,0},{6,3},{7,2},{8,13},{9,12},{10,... | collective-permute-start | bytes 589832 | tf_op jit(solution)/shard_map/ppermute | solution.py:290
  6.0 2.5 %copy-start.1 = (bf16[256,384]{1,0:T(8,128)(2,1)S(1)}, bf16[256,384]{1,0:T(8,128)(2,1)}, u32[]{:S(2)}) copy-start(bf16[256,384]{1,0:T(8,128)(2,1)} %own_ref.3) | copy-start | bytes 589828
  9.8 5.1 %collective-permute-start.2 = (bf16[216,256]{1,0:T(8,128)(2,1)S(1)}, bf16[216,256]{1,0:T(8,128)(2,1)S(1)}, u32[]{:S(2)}, u32[]{:S(2)}) collective-permute-start(bf16[216,256]{1,0:T(8,128)(2,1)S(1)} %get-tuple-element.20), channel_id=1, source_target_pairs={{0,3},{1,2},{2,1},{3,0},{4,7},{5,6},{6,5},{7,4},{8,11},{9,10},{10,... | collective-permute-start | bytes 331784 | tf_op jit(solution)/shard_map/ppermute | solution.py:330
  15.0 1.4 %collective-permute-start.3 = (bf16[192,256]{1,0:T(8,128)(2,1)S(1)}, bf16[192,256]{1,0:T(8,128)(2,1)S(1)}, u32[]{:S(2)}, u32[]{:S(2)}) collective-permute-start(bf16[192,256]{1,0:T(8,128)(2,1)S(1)} %shard_map.103.own_ref), channel_id=1, source_target_pairs={{0,1},{1,0},{2,3},{3,2},{4,5},{5,4},{6,7},{7,6},{8,9},{9,8},{10,11... | collective-permute-start | bytes 294920 | tf_op jit(solution)/shard_map/ppermute | solution.py:332

commit v7 on v6

--- a/solution.py
+++ b/solution.py
@@ -177,8 +177,8 @@
     block_a = jnp.where(local, own_ref[pl.ds(first, blk), :], recv_ref[pl.ds(first, blk), :])
     block_b = jnp.where(local, own_ref[pl.ds(second, blk), :], recv_ref[pl.ds(second, blk), :])
     gain = gain_ref[...][None, :]
-    tokens = jnp.concatenate([block_a, block_b], axis=0)
-    normed = layer_norm(tokens, gain)
+    parts = [layer_norm(block, gain) for block in (block_a, block_b)]
+    normed = jnp.concatenate(parts, axis=0)
     k_t = lax.dot_general(wkv_ref[:hd, :], normed, NT, preferred_element_type=F32)
     v_t = lax.dot_general(wkv_ref[hd:, :], normed, NT, preferred_element_type=F32)
     key_t = jnp.concatenate([k_t.astype(BF16), bar_ref[...]], axis=0)

time: 17.3 us -> 17.4 us (level)
  no operation moved by 1% of the time
where the time goes in v7:
time: 17.4 us; the launch traced here: 17.2 us
  waiting for transfers between devices  7.26 us (42%)
  Pallas kernels  5.19 us (30%)
  starting transfers between devices  4.69 us (27%)
    pallas_call x5, Pallas kernels, call(): pl.pallas_call(kernel, out_shape=tuple(outs), in_specs=[source] * len(arg...  5.19 us
    ppermute x1, waiting for transfers between devices, paired_plan(): recv = lax.ppermute(send, 'col', swap_chip)  3.73 us
    ppermute x1, starting transfers between devices, paired_plan(): single_in = lax.ppermute(single, ('row', 'col'), swap_row)  2.62 us
    ppermute x1, waiting for transfers between devices, paired_plan(): single_in = lax.ppermute(single, ('row', 'col'), swap_row)  2.35 us
    ppermute x1, starting transfers between devices, paired_plan(): recv = lax.ppermute(send, 'col', swap_chip)  1.4 us
    ppermute x1, waiting for transfers between devices, paired_plan(): gated_oth = lax.ppermute(gated_own, 'col', swap_core)  1.18 us
    ppermute x1, starting transfers between devices, paired_plan(): bias_in = lax.ppermute(pair_bias, 'col', swap_core)  0.49 us
  transfers between devices with their start and end apart: 4, of which 3 were waited for; matrix products, arithmetic and copies ran while one was open for 0% of the time, Pallas kernels for 18%

profile of v7, /device:TPU:0, one launch (start us, length us, event | category | flops | bytes accessed | tf_op | source)
XLA Modules:
  0.0 17.2 jit_solution(7541823418169687590)
XLA Ops:
  0.0 0.0 copy-start
  0.0 0.5 %collective-permute-start.1 = (bf16[16,256,128]{2,1,0:T(8,128)(2,1)}, bf16[16,256,128]{2,1,0:T(8,128)(2,1)S(1)}, u32[]{:S(2)}, u32[]{:S(2)}) collective-permute-start(bf16[16,256,128]{2,1,0:T(8,128)(2,1)} %own_ref.2), channel_id=1, source_target_pairs={{0,1},{1,0},{2,3},{3,2},{4,5},{5,4},{6,7},{7,6},{8,9},{9,8},{10,11... | collective-permute-start | bytes 3145736 | tf_op jit(solution)/shard_map/ppermute | solution.py:291
  0.5 2.6 %collective-permute-start = (bf16[256,384]{1,0:T(8,128)(2,1)}, bf16[256,384]{1,0:T(8,128)(2,1)S(1)}, u32[]{:S(2)}, u32[]{:S(2)}) collective-permute-start(bf16[256,384]{1,0:T(8,128)(2,1)} %own_ref.3), channel_id=1, source_target_pairs={{0,5},{1,4},{2,7},{3,6},{4,1},{5,0},{6,3},{7,2},{8,13},{9,12},{10,... | collective-permute-start | bytes 589832 | tf_op jit(solution)/shard_map/ppermute | solution.py:290
  3.1 2.9 %shard_map.100 = (bf16[8,256,208]{2,1,0:T(8,128)(2,1)S(1)}, f32[192,256]{1,0:T(8,128)S(1)}, bf16[384,384]{1,0:T(8,128)(2,1)S(1)}, bf16[96,192]{1,0:T(8,128)(2,1)...) custom-call(bf16[256,384]{1,0:T(8,128)(2,1)} %own_ref.3, ...), custom_call_target="tpu_custom_call" | custom-call | flops 150994944 | bytes 2980352 | tf_op jit(solution)/shard_map/pallas_call | solution.py:266
  6.0 0.0 copy-start.1
  6.0 0.0 collective-permute-done.1.other_ref
  6.0 0.0 copy-done
  6.0 0.2 shard_map.101.bias_ref
  6.2 2.3 %collective-permute-done.recv_ref = bf16[256,384]{1,0:T(8,128)(2,1)S(1)} collective-permute-done((bf16[256,384]{1,0:T(8,128)(2,1)}, bf16[256,384]{1,0:T(8,128)(2,1)S(1)}, u32[]{:S(2)}, u32[]{:S(2)}) %collective-permute-start) | collective-permute-done | bytes 196640 | tf_op jit(solution)/shard_map/ppermute | solution.py:290
  8.5 0.0 copy-done.1
  8.5 1.3 %shard_map.102 = (bf16[216,256]{1,0:T(8,128)(2,1)S(1)}, f32[192,256]{1,0:T(8,128)S(1)}, f32[8,256]{1,0:T(8,128)S(1)}) custom-call(bf16[256,384]{1,0:T(8,128)(2,1)S(1)} %collective-permute-done.recv_ref, bf16[256,384]{1,0:T(8,128)(2,1)S(1)} %copy-done.1, f32[384]{0:T(512)S(1)} %get-tuple-element.16.gain_ref, bf16[384,384]{1,0:T(8,128)(2,1)S(1)} %get-tuple-element.17.wkv_ref, ...), custom_call_target="tpu_custom_call" | custom-call | flops 150994944 | bytes 3962368 | tf_op jit(solution)/shard_map/pallas_call | solution.py:266
  9.8 1.4 %collective-permute-start.2 = (bf16[216,256]{1,0:T(8,128)(2,1)S(1)}, bf16[216,256]{1,0:T(8,128)(2,1)S(1)}, u32[]{:S(2)}, u32[]{:S(2)}) collective-permute-start(bf16[216,256]{1,0:T(8,128)(2,1)S(1)} %get-tuple-element.20), channel_id=1, source_target_pairs={{0,3},{1,2},{2,1},{3,0},{4,7},{5,6},{6,5},{7,4},{8,11},{9,10},{10,... | collective-permute-start | bytes 331784 | tf_op jit(solution)/shard_map/ppermute | solution.py:330
  11.2 3.7 %collective-permute-done.2.recv_ref = bf16[216,256]{1,0:T(8,128)(2,1)S(1)} collective-permute-done((bf16[216,256]{1,0:T(8,128)(2,1)S(1)}, bf16[216,256]{1,0:T(8,128)(2,1)S(1)}, u32[]{:S(2)}, u32[]{:S(2)}) %collective-permute-start.2) | collective-permute-done | bytes 110624 | tf_op jit(solution)/shard_map/ppermute | solution.py:330
  15.0 0.1 shard_map.103.own_ref
  15.0 0.2 %collective-permute-start.3 = (bf16[192,256]{1,0:T(8,128)(2,1)S(1)}, bf16[192,256]{1,0:T(8,128)(2,1)S(1)}, u32[]{:S(2)}, u32[]{:S(2)}) collective-permute-start(bf16[192,256]{1,0:T(8,128)(2,1)S(1)} %shard_map.103.own_ref), channel_id=1, source_target_pairs={{0,1},{1,0},{2,3},{3,2},{4,5},{5,4},{6,7},{7,6},{8,9},{9,8},{10,11... | collective-permute-start | bytes 294920 | tf_op jit(solution)/shard_map/ppermute | solution.py:332
  15.2 1.2 %collective-permute-done.3.oth_ref = bf16[192,256]{1,0:T(8,128)(2,1)S(1)} collective-permute-done((bf16[192,256]{1,0:T(8,128)(2,1)S(1)}, bf16[192,256]{1,0:T(8,128)(2,1)S(1)}, u32[]{:S(2)}, u32[]{:S(2)}) %collective-permute-start.3) | collective-permute-done | bytes 98336 | tf_op jit(solution)/shard_map/ppermute | solution.py:332
  16.4 0.8 %shard_map.104 = f32[96,256]{1,0:T(8,128)} custom-call(bf16[192,256]{1,0:T(8,128)(2,1)S(1)} %shard_map.103.own_ref, bf16[192,256]{1,0:T(8,128)(2,1)S(1)} %collective-permute-done.3.oth_ref, bf16[96,192]{1,0:T(8,128)(2,1)S(1)} %get-tuple-element.24.wo_own_ref, bf16[96,192]{1,0:T(8,128)(2,1)S(1)} %get-tuple-element.25.wo_oth_ref, ...), custom_call_target="tpu_custom_call" | custom-call | flops 18874368 | bytes 466944 | tf_op jit(solution)/shard_map/pallas_call | solution.py:266
Async XLA Ops:
  0.0 6.0 %copy-start = (bf16[16,256,128]{2,1,0:T(8,128)(2,1)S(1)}, bf16[16,256,128]{2,1,0:T(8,128)(2,1)}, u32[]{:S(2)}) copy-start(bf16[16,256,128]{2,1,0:T(8,128)(2,1)} %own_ref.2) | copy-start | bytes 3145732
  0.0 6.0 %collective-permute-start.1 = (bf16[16,256,128]{2,1,0:T(8,128)(2,1)}, bf16[16,256,128]{2,1,0:T(8,128)(2,1)S(1)}, u32[]{:S(2)}, u32[]{:S(2)}) collective-permute-start(bf16[16,256,128]{2,1,0:T(8,128)(2,1)} %own_ref.2), channel_id=1, source_target_pairs={{0,1},{1,0},{2,3},{3,2},{4,5},{5,4},{6,7},{7,6},{8,9},{9,8},{10,11... | collective-permute-start | bytes 3145736 | tf_op jit(solution)/shard_map/ppermute | solution.py:291
  0.5 8.0 %collective-permute-start = (bf16[256,384]{1,0:T(8,128)(2,1)}, bf16[256,384]{1,0:T(8,128)(2,1)S(1)}, u32[]{:S(2)}, u32[]{:S(2)}) collective-permute-start(bf16[256,384]{1,0:T(8,128)(2,1)} %own_ref.3), channel_id=1, source_target_pairs={{0,5},{1,4},{2,7},{3,6},{4,1},{5,0},{6,3},{7,2},{8,13},{9,12},{10,... | collective-permute-start | bytes 589832 | tf_op jit(solution)/shard_map/ppermute | solution.py:290
  6.0 2.5 %copy-start.1 = (bf16[256,384]{1,0:T(8,128)(2,1)S(1)}, bf16[256,384]{1,0:T(8,128)(2,1)}, u32[]{:S(2)}) copy-start(bf16[256,384]{1,0:T(8,128)(2,1)} %own_ref.3) | copy-start | bytes 589828
  9.8 5.1 %collective-permute-start.2 = (bf16[216,256]{1,0:T(8,128)(2,1)S(1)}, bf16[216,256]{1,0:T(8,128)(2,1)S(1)}, u32[]{:S(2)}, u32[]{:S(2)}) collective-permute-start(bf16[216,256]{1,0:T(8,128)(2,1)S(1)} %get-tuple-element.20), channel_id=1, source_target_pairs={{0,3},{1,2},{2,1},{3,0},{4,7},{5,6},{6,5},{7,4},{8,11},{9,10},{10,... | collective-permute-start | bytes 331784 | tf_op jit(solution)/shard_map/ppermute | solution.py:330
  15.0 1.4 %collective-permute-start.3 = (bf16[192,256]{1,0:T(8,128)(2,1)S(1)}, bf16[192,256]{1,0:T(8,128)(2,1)S(1)}, u32[]{:S(2)}, u32[]{:S(2)}) collective-permute-start(bf16[192,256]{1,0:T(8,128)(2,1)S(1)} %shard_map.103.own_ref), channel_id=1, source_target_pairs={{0,1},{1,0},{2,3},{3,2},{4,5},{5,4},{6,7},{7,6},{8,9},{9,8},{10,11... | collective-permute-start | bytes 294920 | tf_op jit(solution)/shard_map/ppermute | solution.py:332

commit v8 on v7

--- a/solution.py
+++ b/solution.py
@@ -249,11 +249,13 @@
     gated_ref[...] = jnp.concatenate(pieces, axis=0).astype(BF16)
 
 
-def project_kernel(own_ref, oth_ref, wo_own_ref, wo_oth_ref, res_ref, out_ref):
-    out_ref[...] = (
-        res_ref[...]
-        + jnp.dot(wo_own_ref[...], own_ref[...], preferred_element_type=F32)
-        + jnp.dot(wo_oth_ref[...], oth_ref[...], preferred_element_type=F32)
+def own_project_kernel(own_ref, wo_own_ref, res_ref, acc_ref):
+    acc_ref[...] = res_ref[...] + jnp.dot(wo_own_ref[...], own_ref[...], preferred_element_type=F32)
+
+
+def project_kernel(acc_ref, oth_ref, wo_oth_ref, out_ref):
+    out_ref[...] = acc_ref[...] + jnp.dot(
+        wo_oth_ref[...], oth_ref[...], preferred_element_type=F32
     )
 
 
@@ -330,11 +332,14 @@
     recv = lax.ppermute(send, "col", swap_chip)
     (gated_own,) = call(merge_kernel, [shape((hd, n), BF16)], (recv, att, lse, gate), flops=n * D)
     gated_oth = lax.ppermute(gated_own, "col", swap_core)
+    (acc,) = call(
+        own_project_kernel,
+        [shape((width, n), F32)],
+        (gated_own, wo_own, res),
+        flops=n * D * width,
+    )
     (out,) = call(
-        project_kernel,
-        [shape((width, n), F32)],
-        (gated_own, gated_oth, wo_own, wo_oth, res),
-        flops=2 * n * D * width,
+        project_kernel, [shape((width, n), F32)], (acc, gated_oth, wo_oth), flops=n * D * width
     )
     return out.T
 

time: 17.4 us -> 17.3 us (level)
    pallas_call x5 -> x6, Pallas kernels: 5.19 us -> 5.31 us  [call(): pl.pallas_call(kernel, out_shape=tuple(outs), in_specs=[source] * len(arg...]
where the time goes in v8:
time: 17.3 us; the launch traced here: 17.2 us
  waiting for transfers between devices  7.11 us (41%)
  Pallas kernels  5.31 us (31%)
  starting transfers between devices  4.69 us (27%)
    pallas_call x6, Pallas kernels, call(): pl.pallas_call(kernel, out_shape=tuple(outs), in_specs=[source] * len(arg...  5.31 us
    ppermute x1, waiting for transfers between devices, paired_plan(): recv = lax.ppermute(send, 'col', swap_chip)  3.73 us
    ppermute x1, starting transfers between devices, paired_plan(): single_in = lax.ppermute(single, ('row', 'col'), swap_row)  2.62 us
    ppermute x1, waiting for transfers between devices, paired_plan(): single_in = lax.ppermute(single, ('row', 'col'), swap_row)  2.35 us
    ppermute x1, starting transfers between devices, paired_plan(): recv = lax.ppermute(send, 'col', swap_chip)  1.4 us
    ppermute x1, waiting for transfers between devices, paired_plan(): gated_oth = lax.ppermute(gated_own, 'col', swap_core)  1.03 us
    ppermute x1, starting transfers between devices, paired_plan(): bias_in = lax.ppermute(pair_bias, 'col', swap_core)  0.49 us
  transfers between devices with their start and end apart: 4, of which 3 were waited for; matrix products, arithmetic and copies ran while one was open for 0% of the time, Pallas kernels for 18%

profile of v8, /device:TPU:0, one launch (start us, length us, event | category | flops | bytes accessed | tf_op | source)
XLA Modules:
  0.0 17.2 jit_solution(847471875884319630)
XLA Ops:
  0.0 0.0 copy-start
  0.0 0.5 %collective-permute-start.1 = (bf16[16,256,128]{2,1,0:T(8,128)(2,1)}, bf16[16,256,128]{2,1,0:T(8,128)(2,1)S(1)}, u32[]{:S(2)}, u32[]{:S(2)}) collective-permute-start(bf16[16,256,128]{2,1,0:T(8,128)(2,1)} %own_ref.2), channel_id=1, source_target_pairs={{0,1},{1,0},{2,3},{3,2},{4,5},{5,4},{6,7},{7,6},{8,9},{9,8},{10,11... | collective-permute-start | bytes 3145736 | tf_op jit(solution)/shard_map/ppermute | solution.py:293
  0.5 2.6 %collective-permute-start = (bf16[256,384]{1,0:T(8,128)(2,1)}, bf16[256,384]{1,0:T(8,128)(2,1)S(1)}, u32[]{:S(2)}, u32[]{:S(2)}) collective-permute-start(bf16[256,384]{1,0:T(8,128)(2,1)} %own_ref.3), channel_id=1, source_target_pairs={{0,5},{1,4},{2,7},{3,6},{4,1},{5,0},{6,3},{7,2},{8,13},{9,12},{10,... | collective-permute-start | bytes 589832 | tf_op jit(solution)/shard_map/ppermute | solution.py:292
  3.1 2.9 %shard_map.100 = (bf16[8,256,208]{2,1,0:T(8,128)(2,1)S(1)}, f32[192,256]{1,0:T(8,128)S(1)}, bf16[384,384]{1,0:T(8,128)(2,1)S(1)}, bf16[96,192]{1,0:T(8,128)(2,1)...) custom-call(bf16[256,384]{1,0:T(8,128)(2,1)} %own_ref.3, ...), custom_call_target="tpu_custom_call" | custom-call | flops 150994944 | bytes 2980352 | tf_op jit(solution)/shard_map/pallas_call | solution.py:268
  6.0 0.0 copy-start.1
  6.0 0.0 collective-permute-done.1.other_ref
  6.0 0.0 copy-done
  6.0 0.2 shard_map.101.bias_ref
  6.2 2.3 %collective-permute-done.recv_ref = bf16[256,384]{1,0:T(8,128)(2,1)S(1)} collective-permute-done((bf16[256,384]{1,0:T(8,128)(2,1)}, bf16[256,384]{1,0:T(8,128)(2,1)S(1)}, u32[]{:S(2)}, u32[]{:S(2)}) %collective-permute-start) | collective-permute-done | bytes 196640 | tf_op jit(solution)/shard_map/ppermute | solution.py:292
  8.5 0.0 copy-done.1
  8.5 1.3 %shard_map.102 = (bf16[216,256]{1,0:T(8,128)(2,1)S(1)}, f32[192,256]{1,0:T(8,128)S(1)}, f32[8,256]{1,0:T(8,128)S(1)}) custom-call(bf16[256,384]{1,0:T(8,128)(2,1)S(1)} %collective-permute-done.recv_ref, bf16[256,384]{1,0:T(8,128)(2,1)S(1)} %copy-done.1, f32[384]{0:T(512)S(1)} %get-tuple-element.16.gain_ref, bf16[384,384]{1,0:T(8,128)(2,1)S(1)} %get-tuple-element.17.wkv_ref, ...), custom_call_target="tpu_custom_call" | custom-call | flops 150994944 | bytes 3962368 | tf_op jit(solution)/shard_map/pallas_call | solution.py:268
  9.8 1.4 %collective-permute-start.2 = (bf16[216,256]{1,0:T(8,128)(2,1)S(1)}, bf16[216,256]{1,0:T(8,128)(2,1)S(1)}, u32[]{:S(2)}, u32[]{:S(2)}) collective-permute-start(bf16[216,256]{1,0:T(8,128)(2,1)S(1)} %get-tuple-element.20), channel_id=1, source_target_pairs={{0,3},{1,2},{2,1},{3,0},{4,7},{5,6},{6,5},{7,4},{8,11},{9,10},{10,... | collective-permute-start | bytes 331784 | tf_op jit(solution)/shard_map/ppermute | solution.py:332
  11.2 3.7 %collective-permute-done.2.recv_ref = bf16[216,256]{1,0:T(8,128)(2,1)S(1)} collective-permute-done((bf16[216,256]{1,0:T(8,128)(2,1)S(1)}, bf16[216,256]{1,0:T(8,128)(2,1)S(1)}, u32[]{:S(2)}, u32[]{:S(2)}) %collective-permute-start.2) | collective-permute-done | bytes 110624 | tf_op jit(solution)/shard_map/ppermute | solution.py:332
  15.0 0.1 shard_map.103.own_ref
  15.0 0.2 %collective-permute-start.3 = (bf16[192,256]{1,0:T(8,128)(2,1)S(1)}, bf16[192,256]{1,0:T(8,128)(2,1)S(1)}, u32[]{:S(2)}, u32[]{:S(2)}) collective-permute-start(bf16[192,256]{1,0:T(8,128)(2,1)S(1)} %shard_map.103.own_ref), channel_id=1, source_target_pairs={{0,1},{1,0},{2,3},{3,2},{4,5},{5,4},{6,7},{7,6},{8,9},{9,8},{10,11... | collective-permute-start | bytes 294920 | tf_op jit(solution)/shard_map/ppermute | solution.py:334
  15.2 0.1 shard_map.104.acc_ref
  15.4 1.0 %collective-permute-done.3.oth_ref = bf16[192,256]{1,0:T(8,128)(2,1)S(1)} collective-permute-done((bf16[192,256]{1,0:T(8,128)(2,1)S(1)}, bf16[192,256]{1,0:T(8,128)(2,1)S(1)}, u32[]{:S(2)}, u32[]{:S(2)}) %collective-permute-start.3) | collective-permute-done | bytes 98336 | tf_op jit(solution)/shard_map/ppermute | solution.py:334
  16.4 0.8 %shard_map.105 = f32[96,256]{1,0:T(8,128)} custom-call(f32[96,256]{1,0:T(8,128)S(1)} %shard_map.104.acc_ref, bf16[192,256]{1,0:T(8,128)(2,1)S(1)} %collective-permute-done.3.oth_ref, bf16[96,192]{1,0:T(8,128)(2,1)S(1)} %get-tuple-element.26.wo_oth_ref), custom_call_target="tpu_custom_call" | custom-call | flops 9437184 | bytes 331776 | tf_op jit(solution)/shard_map/pallas_call | solution.py:268
Async XLA Ops:
  0.0 6.0 %copy-start = (bf16[16,256,128]{2,1,0:T(8,128)(2,1)S(1)}, bf16[16,256,128]{2,1,0:T(8,128)(2,1)}, u32[]{:S(2)}) copy-start(bf16[16,256,128]{2,1,0:T(8,128)(2,1)} %own_ref.2) | copy-start | bytes 3145732
  0.0 6.0 %collective-permute-start.1 = (bf16[16,256,128]{2,1,0:T(8,128)(2,1)}, bf16[16,256,128]{2,1,0:T(8,128)(2,1)S(1)}, u32[]{:S(2)}, u32[]{:S(2)}) collective-permute-start(bf16[16,256,128]{2,1,0:T(8,128)(2,1)} %own_ref.2), channel_id=1, source_target_pairs={{0,1},{1,0},{2,3},{3,2},{4,5},{5,4},{6,7},{7,6},{8,9},{9,8},{10,11... | collective-permute-start | bytes 3145736 | tf_op jit(solution)/shard_map/ppermute | solution.py:293
  0.5 8.0 %collective-permute-start = (bf16[256,384]{1,0:T(8,128)(2,1)}, bf16[256,384]{1,0:T(8,128)(2,1)S(1)}, u32[]{:S(2)}, u32[]{:S(2)}) collective-permute-start(bf16[256,384]{1,0:T(8,128)(2,1)} %own_ref.3), channel_id=1, source_target_pairs={{0,5},{1,4},{2,7},{3,6},{4,1},{5,0},{6,3},{7,2},{8,13},{9,12},{10,... | collective-permute-start | bytes 589832 | tf_op jit(solution)/shard_map/ppermute | solution.py:292
  6.0 2.5 %copy-start.1 = (bf16[256,384]{1,0:T(8,128)(2,1)S(1)}, bf16[256,384]{1,0:T(8,128)(2,1)}, u32[]{:S(2)}) copy-start(bf16[256,384]{1,0:T(8,128)(2,1)} %own_ref.3) | copy-start | bytes 589828
  9.8 5.1 %collective-permute-start.2 = (bf16[216,256]{1,0:T(8,128)(2,1)S(1)}, bf16[216,256]{1,0:T(8,128)(2,1)S(1)}, u32[]{:S(2)}, u32[]{:S(2)}) collective-permute-start(bf16[216,256]{1,0:T(8,128)(2,1)S(1)} %get-tuple-element.20), channel_id=1, source_target_pairs={{0,3},{1,2},{2,1},{3,0},{4,7},{5,6},{6,5},{7,4},{8,11},{9,10},{10,... | collective-permute-start | bytes 331784 | tf_op jit(solution)/shard_map/ppermute | solution.py:332
  15.0 1.4 %collective-permute-start.3 = (bf16[192,256]{1,0:T(8,128)(2,1)S(1)}, bf16[192,256]{1,0:T(8,128)(2,1)S(1)}, u32[]{:S(2)}, u32[]{:S(2)}) collective-permute-start(bf16[192,256]{1,0:T(8,128)(2,1)S(1)} %shard_map.103.own_ref), channel_id=1, source_target_pairs={{0,1},{1,0},{2,3},{3,2},{4,5},{5,4},{6,7},{7,6},{8,9},{9,8},{10,11... | collective-permute-start | bytes 294920 | tf_op jit(solution)/shard_map/ppermute | solution.py:334

commit v9 on v8

--- a/solution.py
+++ b/solution.py
@@ -253,13 +253,22 @@
     acc_ref[...] = res_ref[...] + jnp.dot(wo_own_ref[...], own_ref[...], preferred_element_type=F32)
 
 
-def project_kernel(acc_ref, oth_ref, wo_oth_ref, out_ref):
-    out_ref[...] = acc_ref[...] + jnp.dot(
-        wo_oth_ref[...], oth_ref[...], preferred_element_type=F32
-    )
-
-
-def call(kernel, outs, args, scratch=(), flops=0, trans=0, fetch=False):
+def project_kernel(acc_ref, oth_ref, wo_oth_ref, out_hbm, buf_ref, sems):
+    step = buf_ref.shape[0] // 2
+    copies = []
+    for i in range(2):
+        rows = slice(i * step, (i + 1) * step)
+        buf_ref[rows, :] = acc_ref[rows, :] + jnp.dot(
+            wo_oth_ref[rows, :], oth_ref[...], preferred_element_type=F32
+        )
+        copy = pltpu.make_async_copy(buf_ref.at[rows, :], out_hbm.at[rows, :], sems.at[i])
+        copy.start()
+        copies.append(copy)
+    for copy in copies:
+        copy.wait()
+
+
+def call(kernel, outs, args, scratch=(), flops=0, trans=0, fetch=False, out_space=pltpu.VMEM):
     vmem = pl.BlockSpec(memory_space=pltpu.VMEM)
     source = pl.BlockSpec(memory_space=pltpu.HBM) if fetch else vmem
     if fetch:
@@ -269,7 +278,7 @@
         kernel,
         out_shape=tuple(outs),
         in_specs=[source] * len(args),
-        out_specs=tuple([vmem] * len(outs)),
+        out_specs=tuple([pl.BlockSpec(memory_space=out_space)] * len(outs)),
         scratch_shapes=list(scratch),
         cost_estimate=pl.CostEstimate(flops=flops, bytes_accessed=nbytes, transcendentals=trans),
         compiler_params=pltpu.CompilerParams(vmem_limit_bytes=16 << 20),
@@ -339,7 +348,12 @@
         flops=n * D * width,
     )
     (out,) = call(
-        project_kernel, [shape((width, n), F32)], (acc, gated_oth, wo_oth), flops=n * D * width
+        project_kernel,
+        [shape((width, n), F32)],
+        (acc, gated_oth, wo_oth),
+        [pltpu.VMEM((width, n), F32), pltpu.SemaphoreType.DMA((2,))],
+        flops=n * D * width,
+        out_space=pltpu.HBM,
     )
     return out.T
 

time: 17.3 us -> 17.3 us (level)
  no operation moved by 1% of the time
where the time goes in v9:
time: 17.3 us; the launch traced here: 17.2 us
  waiting for transfers between devices  7.11 us (41%)
  Pallas kernels  5.32 us (31%)
  starting transfers between devices  4.69 us (27%)
    pallas_call x6, Pallas kernels, call(): pl.pallas_call(kernel, out_shape=tuple(outs), in_specs=[source] * len(arg...  5.32 us
    ppermute x1, waiting for transfers between devices, paired_plan(): recv = lax.ppermute(send, 'col', swap_chip)  3.73 us
    ppermute x1, starting transfers between devices, paired_plan(): single_in = lax.ppermute(single, ('row', 'col'), swap_row)  2.62 us
    ppermute x1, waiting for transfers between devices, paired_plan(): single_in = lax.ppermute(single, ('row', 'col'), swap_row)  2.35 us
    ppermute x1, starting transfers between devices, paired_plan(): recv = lax.ppermute(send, 'col', swap_chip)  1.4 us
    ppermute x1, waiting for transfers between devices, paired_plan(): gated_oth = lax.ppermute(gated_own, 'col', swap_core)  1.03 us
    ppermute x1, starting transfers between devices, paired_plan(): bias_in = lax.ppermute(pair_bias, 'col', swap_core)  0.49 us
  transfers between devices with their start and end apart: 4, of which 3 were waited for; matrix products, arithmetic and copies ran while one was open for 0% of the time, Pallas kernels for 18%

profile of v9, /device:TPU:0, one launch (start us, length us, event | category | flops | bytes accessed | tf_op | source)
XLA Modules:
  0.0 17.2 jit_solution(13972982269116794474)
XLA Ops:
  0.0 0.0 copy-start
  0.0 0.5 %collective-permute-start.1 = (bf16[16,256,128]{2,1,0:T(8,128)(2,1)}, bf16[16,256,128]{2,1,0:T(8,128)(2,1)S(1)}, u32[]{:S(2)}, u32[]{:S(2)}) collective-permute-start(bf16[16,256,128]{2,1,0:T(8,128)(2,1)} %own_ref.2), channel_id=1, source_target_pairs={{0,1},{1,0},{2,3},{3,2},{4,5},{5,4},{6,7},{7,6},{8,9},{9,8},{10,11... | collective-permute-start | bytes 3145736 | tf_op jit(solution)/shard_map/ppermute | solution.py:302
  0.5 2.6 %collective-permute-start = (bf16[256,384]{1,0:T(8,128)(2,1)}, bf16[256,384]{1,0:T(8,128)(2,1)S(1)}, u32[]{:S(2)}, u32[]{:S(2)}) collective-permute-start(bf16[256,384]{1,0:T(8,128)(2,1)} %own_ref.3), channel_id=1, source_target_pairs={{0,5},{1,4},{2,7},{3,6},{4,1},{5,0},{6,3},{7,2},{8,13},{9,12},{10,... | collective-permute-start | bytes 589832 | tf_op jit(solution)/shard_map/ppermute | solution.py:301
  3.1 2.9 %shard_map.100 = (bf16[8,256,208]{2,1,0:T(8,128)(2,1)S(1)}, f32[192,256]{1,0:T(8,128)S(1)}, bf16[384,384]{1,0:T(8,128)(2,1)S(1)}, bf16[96,192]{1,0:T(8,128)(2,1)...) custom-call(bf16[256,384]{1,0:T(8,128)(2,1)} %own_ref.3, ...), custom_call_target="tpu_custom_call" | custom-call | flops 150994944 | bytes 2980352 | tf_op jit(solution)/shard_map/pallas_call | solution.py:277
  6.0 0.0 copy-start.1
  6.0 0.0 collective-permute-done.1.other_ref
  6.0 0.0 copy-done
  6.0 0.2 shard_map.101.bias_ref
  6.2 2.3 %collective-permute-done.recv_ref = bf16[256,384]{1,0:T(8,128)(2,1)S(1)} collective-permute-done((bf16[256,384]{1,0:T(8,128)(2,1)}, bf16[256,384]{1,0:T(8,128)(2,1)S(1)}, u32[]{:S(2)}, u32[]{:S(2)}) %collective-permute-start) | collective-permute-done | bytes 196640 | tf_op jit(solution)/shard_map/ppermute | solution.py:301
  8.5 0.0 copy-done.1
  8.5 1.3 %shard_map.102 = (bf16[216,256]{1,0:T(8,128)(2,1)S(1)}, f32[192,256]{1,0:T(8,128)S(1)}, f32[8,256]{1,0:T(8,128)S(1)}) custom-call(bf16[256,384]{1,0:T(8,128)(2,1)S(1)} %collective-permute-done.recv_ref, bf16[256,384]{1,0:T(8,128)(2,1)S(1)} %copy-done.1, f32[384]{0:T(512)S(1)} %get-tuple-element.16.gain_ref, bf16[384,384]{1,0:T(8,128)(2,1)S(1)} %get-tuple-element.17.wkv_ref, ...), custom_call_target="tpu_custom_call" | custom-call | flops 150994944 | bytes 3962368 | tf_op jit(solution)/shard_map/pallas_call | solution.py:277
  9.8 1.4 %collective-permute-start.2 = (bf16[216,256]{1,0:T(8,128)(2,1)S(1)}, bf16[216,256]{1,0:T(8,128)(2,1)S(1)}, u32[]{:S(2)}, u32[]{:S(2)}) collective-permute-start(bf16[216,256]{1,0:T(8,128)(2,1)S(1)} %get-tuple-element.20), channel_id=1, source_target_pairs={{0,3},{1,2},{2,1},{3,0},{4,7},{5,6},{6,5},{7,4},{8,11},{9,10},{10,... | collective-permute-start | bytes 331784 | tf_op jit(solution)/shard_map/ppermute | solution.py:341
  11.2 3.7 %collective-permute-done.2.recv_ref = bf16[216,256]{1,0:T(8,128)(2,1)S(1)} collective-permute-done((bf16[216,256]{1,0:T(8,128)(2,1)S(1)}, bf16[216,256]{1,0:T(8,128)(2,1)S(1)}, u32[]{:S(2)}, u32[]{:S(2)}) %collective-permute-start.2) | collective-permute-done | bytes 110624 | tf_op jit(solution)/shard_map/ppermute | solution.py:341
  15.0 0.1 shard_map.103.own_ref
  15.0 0.2 %collective-permute-start.3 = (bf16[192,256]{1,0:T(8,128)(2,1)S(1)}, bf16[192,256]{1,0:T(8,128)(2,1)S(1)}, u32[]{:S(2)}, u32[]{:S(2)}) collective-permute-start(bf16[192,256]{1,0:T(8,128)(2,1)S(1)} %shard_map.103.own_ref), channel_id=1, source_target_pairs={{0,1},{1,0},{2,3},{3,2},{4,5},{5,4},{6,7},{7,6},{8,9},{9,8},{10,11... | collective-permute-start | bytes 294920 | tf_op jit(solution)/shard_map/ppermute | solution.py:343
  15.2 0.1 shard_map.104.acc_ref
  15.4 1.0 %collective-permute-done.3.oth_ref = bf16[192,256]{1,0:T(8,128)(2,1)S(1)} collective-permute-done((bf16[192,256]{1,0:T(8,128)(2,1)S(1)}, bf16[192,256]{1,0:T(8,128)(2,1)S(1)}, u32[]{:S(2)}, u32[]{:S(2)}) %collective-permute-start.3) | collective-permute-done | bytes 98336 | tf_op jit(solution)/shard_map/ppermute | solution.py:343
  16.4 0.8 %shard_map.105 = f32[96,256]{1,0:T(8,128)} custom-call(f32[96,256]{1,0:T(8,128)S(1)} %shard_map.104.acc_ref, bf16[192,256]{1,0:T(8,128)(2,1)S(1)} %collective-permute-done.3.oth_ref, bf16[96,192]{1,0:T(8,128)(2,1)S(1)} %get-tuple-element.26.wo_oth_ref), custom_call_target="tpu_custom_call" | custom-call | flops 9437184 | bytes 331776 | tf_op jit(solution)/shard_map/pallas_call | solution.py:277
Async XLA Ops:
  0.0 6.0 %copy-start = (bf16[16,256,128]{2,1,0:T(8,128)(2,1)S(1)}, bf16[16,256,128]{2,1,0:T(8,128)(2,1)}, u32[]{:S(2)}) copy-start(bf16[16,256,128]{2,1,0:T(8,128)(2,1)} %own_ref.2) | copy-start | bytes 3145732
  0.0 6.0 %collective-permute-start.1 = (bf16[16,256,128]{2,1,0:T(8,128)(2,1)}, bf16[16,256,128]{2,1,0:T(8,128)(2,1)S(1)}, u32[]{:S(2)}, u32[]{:S(2)}) collective-permute-start(bf16[16,256,128]{2,1,0:T(8,128)(2,1)} %own_ref.2), channel_id=1, source_target_pairs={{0,1},{1,0},{2,3},{3,2},{4,5},{5,4},{6,7},{7,6},{8,9},{9,8},{10,11... | collective-permute-start | bytes 3145736 | tf_op jit(solution)/shard_map/ppermute | solution.py:302
  0.5 8.0 %collective-permute-start = (bf16[256,384]{1,0:T(8,128)(2,1)}, bf16[256,384]{1,0:T(8,128)(2,1)S(1)}, u32[]{:S(2)}, u32[]{:S(2)}) collective-permute-start(bf16[256,384]{1,0:T(8,128)(2,1)} %own_ref.3), channel_id=1, source_target_pairs={{0,5},{1,4},{2,7},{3,6},{4,1},{5,0},{6,3},{7,2},{8,13},{9,12},{10,... | collective-permute-start | bytes 589832 | tf_op jit(solution)/shard_map/ppermute | solution.py:301
  6.0 2.5 %copy-start.1 = (bf16[256,384]{1,0:T(8,128)(2,1)S(1)}, bf16[256,384]{1,0:T(8,128)(2,1)}, u32[]{:S(2)}) copy-start(bf16[256,384]{1,0:T(8,128)(2,1)} %own_ref.3) | copy-start | bytes 589828
  9.8 5.1 %collective-permute-start.2 = (bf16[216,256]{1,0:T(8,128)(2,1)S(1)}, bf16[216,256]{1,0:T(8,128)(2,1)S(1)}, u32[]{:S(2)}, u32[]{:S(2)}) collective-permute-start(bf16[216,256]{1,0:T(8,128)(2,1)S(1)} %get-tuple-element.20), channel_id=1, source_target_pairs={{0,3},{1,2},{2,1},{3,0},{4,7},{5,6},{6,5},{7,4},{8,11},{9,10},{10,... | collective-permute-start | bytes 331784 | tf_op jit(solution)/shard_map/ppermute | solution.py:341
  15.0 1.4 %collective-permute-start.3 = (bf16[192,256]{1,0:T(8,128)(2,1)S(1)}, bf16[192,256]{1,0:T(8,128)(2,1)S(1)}, u32[]{:S(2)}, u32[]{:S(2)}) collective-permute-start(bf16[192,256]{1,0:T(8,128)(2,1)S(1)} %shard_map.103.own_ref), channel_id=1, source_target_pairs={{0,1},{1,0},{2,3},{3,2},{4,5},{5,4},{6,7},{7,6},{8,9},{9,8},{10,11... | collective-permute-start | bytes 294920 | tf_op jit(solution)/shard_map/ppermute | solution.py:343
